TPU v7x, 256 devices: a whole 4x4x8 slice. The times are simulated.
256 devices in a mesh: epoch: 16 (over y, x), sky: 16 (over z, core).
Axes of the slice: x: 4, y: 4, z: 8, core: 2. Of those that a mesh axis runs over, the one named last changes fastest.
Arguments:
- images: float32 [256, 32, 8192], P('epoch', None, 'sky'), may hold values from -6 to 6
- variances: float32 [256, 32, 8192], P('epoch', None, 'sky'), may hold values from 0.25 to 4
- coefficients: bfloat16 [256, 4, 32, 8192], P('epoch', None, None, 'sky'), may hold values from 0.049804688 to 0.5
- row_filters: float32 [256, 4, 11], P('epoch'), may hold values from 0.03 to 0.3
- col_filters: float32 [256, 4, 11], P('epoch'), may hold values from 0.03 to 0.3
- dithers: int32 [256, 2], P('epoch'), may hold values from -3 to 3
Outputs:
- template: float32 [32, 8192], P(None, 'sky')
- mean_weight: float32 [32, 8192], P(None, 'sky')
All inputs are finite; a program needn't handle non-finite values.
Results may differ from a plain program's by a relative error of at most 0.0003.
Values sent between devices are 32-bit elements; how exact they have to be, the bound alone decides.
A program may use at most 128 MiB of HBM per device.

v0:
```python
import jax
import jax.numpy as jnp
from jax import lax
from jax.sharding import PartitionSpec as P

TAPS = 11
REJECT = 4
HALF = 5
HALO = 8


READ_NOISE = 0.25


def extended(shard, sides, width):
    for axis, dim in sides:
        devices, length = (lax.axis_size(axis), shard.shape[dim])
        up = [(i, (i + 1) % devices) for i in range(devices - 1)]
        down = [(j, i) for i, j in up]
        last = lax.slice_in_dim(shard, length - width, length, axis=dim)
        first = lax.slice_in_dim(shard, 0, width, axis=dim)
        before = lax.ppermute(last, axis, up)
        after = lax.ppermute(first, axis, down)
        shard = jnp.concatenate([before, shard, after], axis=dim)
    return shard


def combined_all(value, axis, join):
    pieces = jax.tree.map(lambda part: lax.all_gather(part, axis), value)
    head = jax.tree.map(lambda part: part[0], pieces)
    tail = jax.tree.map(lambda part: part[1:], pieces)
    running, _ = lax.scan(lambda running, piece: (join(running, piece), None), head, tail)
    return running


def cut_window(source, shifts):
    band_rows = source.shape[1] - 2 * HALO
    strip_cols = source.shape[2] - 2 * HALO
    first_row = HALO - HALF - shifts[0]
    first_col = HALO - HALF - shifts[1]
    zero_index = jnp.zeros((), jnp.int32)
    return lax.dynamic_slice(
        source,
        (zero_index, first_row, first_col),
        (source.shape[0], band_rows + 2 * HALF, strip_cols + 2 * HALF),
    )


def smear_all(windows, row_taps, col_taps, coeff_planes):
    band_rows = windows.shape[2] - 2 * HALF
    strip_cols = windows.shape[3] - 2 * HALF
    row_pass = row_taps[:, None, :, 0, None, None] * windows[:, :, None, 0:band_rows, :]
    for offset in range(1, TAPS):
        row_pass = (
            row_pass
            + row_taps[:, None, :, offset, None, None]
            * windows[:, :, None, offset : offset + band_rows, :]
        )
    col_pass = col_taps[:, None, :, 0, None, None] * row_pass[:, :, :, :, 0:strip_cols]
    for offset in range(1, TAPS):
        col_pass = (
            col_pass
            + col_taps[:, None, :, offset, None, None]
            * row_pass[:, :, :, :, offset : offset + strip_cols]
        )
    return jnp.sum(coeff_planes[:, None].astype(jnp.float32) * col_pass, axis=2)


def insert_low(slots, value):
    result = []
    for entry in slots:
        result.append(jnp.minimum(entry, value))
        value = jnp.maximum(entry, value)
    return tuple(result)


def insert_high(slots, value):
    result = list(slots)
    for place in range(len(slots) - 1, -1, -1):
        result[place] = jnp.maximum(slots[place], value)
        value = jnp.minimum(slots[place], value)
    return tuple(result)


def select_ends(stacked):
    blank = jnp.zeros(stacked.shape[1:], jnp.float32)
    low_init = tuple((blank + jnp.inf for place in range(REJECT)))
    high_init = tuple((blank - jnp.inf for place in range(REJECT)))

    def step_one(index, carry):
        value = lax.dynamic_index_in_dim(stacked, index, 0, keepdims=False)
        return (insert_low(carry[0], value), insert_high(carry[1], value))

    low_slots, high_slots = lax.fori_loop(0, stacked.shape[0], step_one, (low_init, high_init))
    return (jnp.stack(low_slots, axis=0), jnp.stack(high_slots, axis=0))


def combine_lists(first_list, second_list):
    low_slots = tuple((first_list[0][place] for place in range(REJECT)))
    high_slots = tuple((first_list[1][place] for place in range(REJECT)))
    for place in range(REJECT):
        low_slots = insert_low(low_slots, second_list[0][place])
        high_slots = insert_high(high_slots, second_list[1][place])
    return (
        jnp.stack(low_slots, axis=0),
        jnp.stack(high_slots, axis=0),
        first_list[2] + second_list[2],
    )


def per_device(images, variances, coefficients, row_filters, col_filters, dithers):
    stacked = jnp.stack([images, variances], axis=1)
    widened = extended(stacked, (("sky", 3),), HALO)
    padded = jnp.pad(widened, ((0, 0), (0, 0), (HALO, HALO), (0, 0)))
    windows = jax.vmap(cut_window)(padded, dithers)
    smeared = smear_all(windows, row_filters, col_filters, coefficients)
    weight = 1.0 / (smeared[:, 1] + READ_NOISE)
    weighted = weight * smeared[:, 0]
    paired = jnp.stack([weighted, weight], axis=1)
    low_ends, high_ends = select_ends(paired)
    totals = jnp.sum(paired, axis=0)
    kept_count = float(paired.shape[0] * lax.axis_size("epoch") - 2 * REJECT)
    merged_low, merged_high, merged_totals = combined_all(
        (low_ends, high_ends, totals), "epoch", combine_lists
    )
    trimmed = merged_totals - jnp.sum(merged_low, axis=0) - jnp.sum(merged_high, axis=0)
    template = trimmed[0] / trimmed[1]
    mean_weight = trimmed[1] / kept_count
    return (template, mean_weight)


def solution(mesh):
    placed = (
        P("epoch", None, "sky"),
        P("epoch", None, "sky"),
        P("epoch", None, None, "sky"),
        P("epoch", None, None),
        P("epoch", None, None),
        P("epoch", None),
    )
    return jax.shard_map(
        per_device,
        mesh=mesh,
        in_specs=placed,
        out_specs=(P(None, "sky"), P(None, "sky")),
        check_vma=False,
    )
```

profile of v0, /device:TPU:2, one launch (start us, length us, event | category | flops | bytes accessed | tf_op | source)
XLA Modules:
  0.0 471.4 jit_solution(13618126992853397287)
XLA Ops:
  44.7 4.1 convert_element_type.6
  52.5 70.3 %while.44 = (s32[]{:T(128)}, f32[16,2,48,528]{3,2,1,0:T(8,128)}, s32[16,4]{0,1:T(4,128)S(1)}, f32[16,2,42,522]{3,2,1,0:T(8,128)}, s32[]{:T(128)}) while((s32[]{:T(128)}, f32[16,2,48,528]{3,2,1,0:T(8,128)}, s32[16,4]{0,1:T(4,128)S(1)}, f32[16,2,42,522]{3,2,1,0:T(8,128)}, s32[]{:T(128)}) %tuple.136), condition=%wide.while_cond, body=%wide.while_body.sunk | while | flops 2 | bytes 493689 | solution.py:42
  53.2 3.7 dynamic-slice_dynamic-update-slice_fusion.2
  57.6 3.7 dynamic-slice_dynamic-update-slice_fusion.2
  62.0 3.7 dynamic-slice_dynamic-update-slice_fusion.2
  66.4 3.7 dynamic-slice_dynamic-update-slice_fusion.2
  70.8 3.7 dynamic-slice_dynamic-update-slice_fusion.2
  79.6 3.7 dynamic-slice_dynamic-update-slice_fusion.2
  83.9 3.7 dynamic-slice_dynamic-update-slice_fusion.2
  92.7 3.7 dynamic-slice_dynamic-update-slice_fusion.2
  97.1 3.7 dynamic-slice_dynamic-update-slice_fusion.2
  105.9 3.7 dynamic-slice_dynamic-update-slice_fusion.2
  110.3 3.7 dynamic-slice_dynamic-update-slice_fusion.2
  114.7 3.7 dynamic-slice_dynamic-update-slice_fusion.2
  122.9 19.9 %fusion.43 = (f32[16,2,32,522]{3,2,1,0:T(8,128)S(1)}, f32[16,2,32,522]{3,2,1,0:T(8,128)S(1)}, f32[16,2,32,522]{3,2,1,0:T(8,128)}, f32[16,2,32,522]{3,2,1,0:T(8,1...) fusion(f32[16,2,42,522]{3,2,1,0:T(8,128)} %get-tuple-element.235), kind=kLoop, calls=%fused_computation.126 | loop fusion | bytes 47038464 | tf_op jit(solution)/shard_map/slice | solution.py:52
  143.0 13.2 %multiply_add_fusion = f32[16,2,4,32,522]{4,3,2,1,0:T(8,128)S(1)} fusion(f32[16,2,32,522]{3,2,1,0:T(8,128)} %get-tuple-element.358, f32[16,4]{1,0:T(8,128)S(1)} %copy-done.23, f32[16,2,32,522]{3,2,1,0:T(8,128)S(1)} %get-tuple-element.349, f32[16,4]{1,0:T(8,128)S(1)} %copy-done.21, f32[16,2,32,522]{3,2,1,0:T(8,128)} %get-tuple-element.350, ...), kind=kLoop, calls=%fused_computation.57 | loop fusion | flops 44900352 | bytes 32074496 | tf_op jit(solution)/shard_map/add | solution.py:55
  156.4 25.5 %fusion.20 = f32[16,2,32,512]{3,2,1,0:T(8,128)S(1)} fusion(f32[16,2,4,32,522]{4,3,2,1,0:T(8,128)S(1)} %multiply_add_fusion, f32[16,4]{1,0:T(8,128)S(1)} %copy-done.24, f32[16,4]{1,0:T(8,128)S(1)} %copy-done.22, f32[16,4]{1,0:T(8,128)S(1)} %copy-done.20, f32[16,4]{1,0:T(8,128)S(1)} %copy-done.18, f32[16,4]{1,0:T(8,128)S(1)} %copy-done.16, ...), kind=kLoop, calls=%fused_computation.61 | loop fusion | flops 47710208 | bytes 98568960 | tf_op jit(solution)/shard_map/reduce_sum | solution.py:66
  183.2 5.5 %while.45 = (s32[]{:T(128)}, f32[2,32,512]{2,1,0:T(8,128)S(1)}, f32[2,32,512]{2,1,0:T(8,128)S(1)}, f32[2,32,512]{2,1,0:T(8,128)S(1)}, f32[2,32,512]{2,1,0:T(8,12...) while((s32[]{:T(128)}, f32[2,32,512]{2,1,0:T(8,128)S(1)}, ...), condition=%wide.region_2.3_spmd.clone, body=%wide.region_1.2_spmd.clone.sunk | while | flops 851971 | bytes 3408004 | solution.py:94
  190.5 49.0 %all-gather.11.cloned.1.call-done = f32[32,32,512]{2,1,0:T(8,128)} async-done(((f32[2,32,512]{2,1,0:T(8,128)}), f32[32,32,512]{2,1,0:T(8,128)}) %all-gather.11.cloned.1.call-update) | async-done | bytes 2097168 | tf_op jit(solution)/shard_map/all_gather | solution.py:29
  241.3 76.2 %all-gather.9.cloned.1.call-done = f32[64,2,32,512]{3,2,1,0:T(8,128)} async-done(((f32[4,2,32,512]{3,2,1,0:T(8,128)}), f32[64,2,32,512]{3,2,1,0:T(8,128)}) %all-gather.9.cloned.1.call-update) | async-done | bytes 8388624 | tf_op jit(solution)/shard_map/all_gather | solution.py:29
  317.5 8.0 %slice.330 = f32[60,2,32,512]{3,2,1,0:T(8,128)} slice(f32[64,2,32,512]{3,2,1,0:T(8,128)} %all-gather.9.cloned.1.call-done), slice={[4:64], [0:2], [0:32], [0:512]} | slice | bytes 15728640 | tf_op jit(solution)/shard_map/slice | solution.py:31
  325.6 69.9 %all-gather.7.cloned.1.call-done = f32[64,2,32,512]{3,2,1,0:T(8,128)} async-done(((f32[4,2,32,512]{3,2,1,0:T(8,128)}), f32[64,2,32,512]{3,2,1,0:T(8,128)}) %all-gather.7.cloned.1.call-update) | async-done | bytes 8388624 | tf_op jit(solution)/shard_map/all_gather | solution.py:29
  395.5 8.1 %slice.329 = f32[60,2,32,512]{3,2,1,0:T(8,128)} slice(f32[64,2,32,512]{3,2,1,0:T(8,128)} %all-gather.7.cloned.1.call-done), slice={[4:64], [0:2], [0:32], [0:512]} | slice | bytes 15728640 | tf_op jit(solution)/shard_map/slice | solution.py:31
  403.6 60.5 %while.43 = (s32[]{:T(128)}, f32[4,2,32,512]{3,2,1,0:T(8,128)S(1)}, f32[4,2,32,512]{3,2,1,0:T(8,128)S(1)}, f32[2,32,512]{2,1,0:T(8,128)S(1)}, f32[15,4,2,32,512]...) while((s32[]{:T(128)}, f32[4,2,32,512]{3,2,1,0:T(8,128)S(1)}, ...), condition=%wide.region_5.6_spmd, body=%wide.region_4.5_spmd.sunk | while | flops 3178501 | bytes 9568457 | solution.py:32
  (318 shorter events, 136.8 us)
Async XLA Ops:
  7.2 41.6 %copy-start.3 = (f32[16,32,512]{2,1,0:T(8,128)S(1)}, f32[16,32,512]{2,1,0:T(8,128)}, u32[]{:S(2)}) copy-start(f32[16,32,512]{2,1,0:T(8,128)} %param.10) | copy-start | bytes 3145732
  7.2 41.6 %copy-start.2 = (f32[16,32,512]{2,1,0:T(8,128)S(1)}, f32[16,32,512]{2,1,0:T(8,128)}, u32[]{:S(2)}) copy-start(f32[16,32,512]{2,1,0:T(8,128)} %param.11) | copy-start | bytes 3145732
  7.2 232.4 %all-gather.11.cloned.1.call-start = ((), (), s32[]{:S(2)}) async-start(), calls=%async_computation.2 | async-start | bytes 2228224 | tf_op jit(solution)/shard_map/all_gather | solution.py:29
  9.8 39.0 %collective-permute-start = (f32[16,2,32,8]{3,2,1,0:T(8,128)}, f32[16,2,32,8]{3,2,1,0:T(8,128)S(1)}, u32[]{:S(2)}, u32[]{:S(2)}) collective-permute-start(f32[16,2,32,8]{3,2,1,0:T(8,128)} %get-tuple-element.363), channel_id=1, source_target_pairs={{0,1},{1,2},{2,3},{3,4},{4,5},{5,6},{6,7},{7,8},{8,9},{9,10},{10,1... | collective-permute-start | bytes 98312 | tf_op jit(solution)/shard_map/ppermute | solution.py:22
  11.5 37.3 %collective-permute-start.1 = (f32[16,2,32,8]{3,2,1,0:T(8,128)}, f32[16,2,32,8]{3,2,1,0:T(8,128)}, u32[]{:S(2)}, u32[]{:S(2)}) collective-permute-start(f32[16,2,32,8]{3,2,1,0:T(8,128)} %get-tuple-element.364), channel_id=1, source_target_pairs={{1,0},{2,1},{3,2},{4,3},{5,4},{6,5},{7,6},{8,7},{9,8},{10,9},{11,1... | collective-permute-start | bytes 98312 | tf_op jit(solution)/shard_map/ppermute | solution.py:23
  122.8 20.0 %copy-start.5 = (f32[16,4]{1,0:T(8,128)S(1)}, f32[16,4]{1,0:T(8,128)}, u32[]{:S(2)}) copy-start(f32[16,4]{1,0:T(8,128)} %copy.54) | copy-start | bytes 772
  122.8 20.0 %copy-start.7 = (f32[16,4]{1,0:T(8,128)S(1)}, f32[16,4]{1,0:T(8,128)}, u32[]{:S(2)}) copy-start(f32[16,4]{1,0:T(8,128)} %copy.55) | copy-start | bytes 772
  122.8 20.0 %copy-start.9 = (f32[16,4]{1,0:T(8,128)S(1)}, f32[16,4]{1,0:T(8,128)}, u32[]{:S(2)}) copy-start(f32[16,4]{1,0:T(8,128)} %copy.56) | copy-start | bytes 772
  122.8 20.0 %copy-start.11 = (f32[16,4]{1,0:T(8,128)S(1)}, f32[16,4]{1,0:T(8,128)}, u32[]{:S(2)}) copy-start(f32[16,4]{1,0:T(8,128)} %copy.57) | copy-start | bytes 772
  122.8 20.0 %copy-start.13 = (f32[16,4]{1,0:T(8,128)S(1)}, f32[16,4]{1,0:T(8,128)}, u32[]{:S(2)}) copy-start(f32[16,4]{1,0:T(8,128)} %copy.58) | copy-start | bytes 772
  122.8 20.0 %copy-start.15 = (f32[16,4]{1,0:T(8,128)S(1)}, f32[16,4]{1,0:T(8,128)}, u32[]{:S(2)}) copy-start(f32[16,4]{1,0:T(8,128)} %copy.59) | copy-start | bytes 772
  122.9 20.0 %copy-start.17 = (f32[16,4]{1,0:T(8,128)S(1)}, f32[16,4]{1,0:T(8,128)}, u32[]{:S(2)}) copy-start(f32[16,4]{1,0:T(8,128)} %copy.60) | copy-start | bytes 772
  122.9 20.0 %copy-start.19 = (f32[16,4]{1,0:T(8,128)S(1)}, f32[16,4]{1,0:T(8,128)}, u32[]{:S(2)}) copy-start(f32[16,4]{1,0:T(8,128)} %copy.61) | copy-start | bytes 772
  122.9 20.0 %copy-start.21 = (f32[16,4]{1,0:T(8,128)S(1)}, f32[16,4]{1,0:T(8,128)}, u32[]{:S(2)}) copy-start(f32[16,4]{1,0:T(8,128)} %copy.62) | copy-start | bytes 772
  122.9 20.0 %copy-start.23 = (f32[16,4]{1,0:T(8,128)S(1)}, f32[16,4]{1,0:T(8,128)}, u32[]{:S(2)}) copy-start(f32[16,4]{1,0:T(8,128)} %copy.63) | copy-start | bytes 772
  142.9 13.3 %copy-start = (f32[16,4,32,512]{3,2,1,0:T(8,128)S(1)}, f32[16,4,32,512]{3,2,1,0:T(8,128)}, u32[]{:S(2)}) copy-start(f32[16,4,32,512]{3,2,1,0:T(8,128)} %convert_element_type.6) | copy-start | bytes 12582916
  142.9 13.3 %copy-start.4 = (f32[16,4]{1,0:T(8,128)S(1)}, f32[16,4]{1,0:T(8,128)}, u32[]{:S(2)}) copy-start(f32[16,4]{1,0:T(8,128)} %copy.52) | copy-start | bytes 772
  142.9 13.3 %copy-start.6 = (f32[16,4]{1,0:T(8,128)S(1)}, f32[16,4]{1,0:T(8,128)}, u32[]{:S(2)}) copy-start(f32[16,4]{1,0:T(8,128)} %copy.64) | copy-start | bytes 772
  142.9 13.3 %copy-start.8 = (f32[16,4]{1,0:T(8,128)S(1)}, f32[16,4]{1,0:T(8,128)}, u32[]{:S(2)}) copy-start(f32[16,4]{1,0:T(8,128)} %copy.65) | copy-start | bytes 772
  142.9 13.3 %copy-start.10 = (f32[16,4]{1,0:T(8,128)S(1)}, f32[16,4]{1,0:T(8,128)}, u32[]{:S(2)}) copy-start(f32[16,4]{1,0:T(8,128)} %copy.66) | copy-start | bytes 772
  183.1 134.4 %all-gather.9.cloned.1.call-start = ((), (), s32[]{:S(2)}) async-start(), calls=%async_computation.1 | async-start | bytes 8912896 | tf_op jit(solution)/shard_map/all_gather | solution.py:29
  189.6 205.9 %all-gather.7.cloned.1.call-start = ((), (), s32[]{:S(2)}) async-start(), calls=%async_computation | async-start | bytes 8912896 | tf_op jit(solution)/shard_map/all_gather | solution.py:29
  325.5 78.0 %slice-start.1 = ((f32[64,2,32,512]{3,2,1,0:T(8,128)}), f32[4,2,32,512]{3,2,1,0:T(8,128)S(1)}, s32[]{:S(2)}) async-start(f32[64,2,32,512]{3,2,1,0:T(8,128)} %all-gather.9.cloned.1.call-done), calls=%async_computation.4 | async-start | bytes 1048576 | tf_op jit(solution)/shard_map/slice | solution.py:30
  325.6 78.0 %slice-start.2 = ((f32[32,32,512]{2,1,0:T(8,128)}), f32[2,32,512]{2,1,0:T(8,128)S(1)}, s32[]{:S(2)}) async-start(f32[32,32,512]{2,1,0:T(8,128)} %all-gather.11.cloned.1.call-done), calls=%async_computation.5 | async-start | bytes 262144 | tf_op jit(solution)/shard_map/slice | solution.py:30
  (9 other events, 102.8 us)
Sparse Core Ops, SparseCore 0:
  183.2 56.2 all-gather.10
  242.0 75.4 all-gather.8
  319.9 75.4 all-gather.6
where the time goes:
time: 475 us; the launch traced here: 471 us
  waiting for transfers between devices  195 us (41%)
  local copies, waits for them, and re-layouts  139 us (29%)
  other arithmetic  118 us (25%)
  between operations  14.3 us (3%)
    all_gather x3, waiting for transfers between devices, combined_all(): pieces = jax.tree.map(lambda part: lax.all_gather(part, axis), value)  195 us
    gather x48, local copies, waits for them, and re-layouts  70.3 us
    max x77, other arithmetic, insert_high(): result[place] = jnp.maximum(slots[place], value)  43.2 us
    reduce_sum x1, other arithmetic, smear_all(): return jnp.sum(coeff_planes[:, None].astype(jnp.float32) * col_pass, axis=2)  25.5 us
    slice x1, local copies, waits for them, and re-layouts, smear_all(): windows[:, :, None, 0:band_rows, :]  19.9 us
    min x30, other arithmetic, insert_low(): result.append(jnp.minimum(entry, value))  19.4 us
    slice x3, local copies, waits for them, and re-layouts, combined_all(): tail = jax.tree.map(lambda part: part[1:], pieces)  17.9 us
    mul x10, local copies, waits for them, and re-layouts, smear_all(): row_taps[:, None, :, offset, None, None]  13.2 us
  transfers between devices with their start and end apart: 5, of which 3 were waited for; matrix products, arithmetic and copies ran while one was open for 11% of the time, Pallas kernels for 0%

commit v1 on v0

v1 whole, which is shorter than its diff:
```python
import jax
import jax.numpy as jnp
from jax import lax
from jax.experimental import pallas as pl
from jax.experimental.pallas import tpu as pltpu
from jax.sharding import PartitionSpec as P

TAPS = 11
BASES = 4
REJECT = 4
HALF = 5
HALO = 8
READ_NOISE = 0.25

LANES = 128
EPOCHS = 16
ROWS = 32
BLOCKS = 4
SIDE = 4
PEERS = SIDE * SIDE
LISTS = 2 * (2 * REJECT + 1)
GROUPS = ((1, 2), (0, 3))
MESH = pl.DeviceIdType.MESH


def split(value):
    high = value.astype(jnp.bfloat16)
    return high, value - high.astype(jnp.float32)


def exchange(first, second):
    return jnp.minimum(first, second), jnp.maximum(first, second)


def sort_four(values):
    a, b, c, d = values
    a, b = exchange(a, b)
    c, d = exchange(c, d)
    a, c = exchange(a, c)
    b, d = exchange(b, d)
    b, c = exchange(b, c)
    return [a, b, c, d]


def sort_bitonic(values):
    a, b, c, d = values
    a, c = exchange(a, c)
    b, d = exchange(b, d)
    a, b = exchange(a, b)
    c, d = exchange(c, d)
    return [a, b, c, d]


def lower_four(first, second):
    return [jnp.minimum(first[i], second[REJECT - 1 - i]) for i in range(REJECT)]


def upper_four(first, second):
    return [jnp.maximum(first[i], second[REJECT - 1 - i]) for i in range(REJECT)]


def merge_ends(first, second, last=False):
    low = lower_four(first[0], second[0])
    high = upper_four(first[1], second[1])
    if not last:
        low, high = sort_bitonic(low), sort_bitonic(high)
    return low, high


def merge_tree(lists):
    while len(lists) > 1:
        last = False
        lists = [merge_ends(lists[i], lists[i + 1], last) for i in range(0, len(lists), 2)]
    return lists[0]


def sum_tree(values):
    values = list(values)
    while len(values) > 1:
        values = [values[i] + values[i + 1] for i in range(0, len(values) - 1, 2)] + (
            [values[-1]] if len(values) % 2 else []
        )
    return values[0]


def kernel(
    img_hbm, var_hbm, coef_hbm, rowf_ref, colf_ref, dith_ref, out_ref,
    img, var, coef, filt, flip, toep, band, pack, halo, val, lists, stage1, mid, stage2, final,
    in_sem, halo_send, halo_recv, s1_send, s1_recv, s2_send, s2_recv, own_sem, fin_send, fin_recv,
):
    me = lax.axis_index("epoch")
    sky = lax.axis_index("sky")
    strips = lax.axis_size("sky")
    my_y, my_x = me // SIDE, me % SIDE
    right, left = (sky + 1) % strips, (sky + strips - 1) % strips

    def peer_at(dy, dx):
        return ((my_y + dy) % SIDE) * SIDE + (my_x + dx) % SIDE

    offsets = [(dy, dx) for dy in range(SIDE) for dx in range(SIDE) if dy or dx]

    barrier = pltpu.get_barrier_semaphore()
    for neighbour in (left, right):
        pl.semaphore_signal(barrier, inc=1, device_id=(me, neighbour), device_id_type=MESH)
    for dy, dx in offsets:
        pl.semaphore_signal(barrier, inc=1, device_id=(peer_at(dy, dx), sky), device_id_type=MESH)

    loads = [
        pltpu.make_async_copy(img_hbm, img, in_sem.at[0]),
        pltpu.make_async_copy(var_hbm, var, in_sem.at[1]),
        pltpu.make_async_copy(coef_hbm, coef, in_sem.at[2]),
    ]
    for load in loads:
        load.start()

    lane8 = lax.broadcasted_iota(jnp.int32, (ROWS, LANES), 1)
    filt[...] = jnp.zeros_like(filt)
    for e in range(EPOCHS):
        filt[0, BASES * e : BASES * (e + 1), 0:TAPS] = rowf_ref[e]
        filt[1, BASES * e : BASES * (e + 1), 0:TAPS] = colf_ref[e]
    tap = lax.broadcasted_iota(jnp.int32, (LANES, LANES), 0)
    place = lax.broadcasted_iota(jnp.int32, (LANES, LANES), 1)
    count = EPOCHS * BASES
    for kind in range(2):
        high, low = split(filt[kind])
        parts = jnp.concatenate([high, low.astype(jnp.bfloat16)], axis=0)
        for turn in range(8):
            target = tap + turn if kind == 0 else TAPS - 1 - tap + turn
            moved = jnp.dot(
                parts,
                jnp.where(place == target, 1.0, 0.0).astype(jnp.bfloat16),
                preferred_element_type=jnp.float32,
            )
            flip[2 * kind, pl.ds(turn, count, stride=8), :] = moved[0:count]
            flip[2 * kind + 1, pl.ds(turn, count, stride=8), :] = moved[count : 2 * count]

    keep = place <= tap
    tail_keep = (place > tap)[0:16]

    def build(e, _):
        row_turn = LANES - HALF - dith_ref[e, 0]
        col_turn = LANES - HALF - HALO + dith_ref[e, 1]
        pad = jnp.zeros((LANES - 48, LANES), jnp.bfloat16)
        for b in range(BASES):
            at = e * BASES + b
            cols = slice(b * LANES, (b + 1) * LANES)

            def turned(which, rows, turn):
                base = flip[which, pl.ds(pl.multiple_of(at * 8, 8), 8), :]
                return jnp.concatenate(
                    [pltpu.roll(base, (turn + g) % LANES, 1) for g in range(0, rows, 8)], axis=0
                )

            high = jnp.where(lane8 < ROWS, turned(0, ROWS, row_turn), 0.0)
            low = jnp.where(lane8 < ROWS, turned(1, ROWS, row_turn), 0.0)
            both = high + pltpu.roll(high, ROWS, 1) + pltpu.roll(low, 2 * ROWS, 1)
            band[e, b] = both.astype(jnp.bfloat16)

            high = turned(2, LANES, col_turn)
            low = turned(3, LANES, col_turn)
            top = jnp.where(keep, high, 0.0).astype(jnp.bfloat16)
            toep[e, 0:LANES, cols] = top
            toep[e, LANES : 2 * LANES, cols] = top
            toep[e, 2 * LANES : 3 * LANES, cols] = jnp.where(keep, low, 0.0).astype(jnp.bfloat16)
            tail = jnp.where(tail_keep, high[0:16], 0.0).astype(jnp.bfloat16)
            toep[e, 3 * LANES : 3 * LANES + 16, cols] = tail
            toep[e, 3 * LANES + 16 : 3 * LANES + 32, cols] = tail
            toep[e, 3 * LANES + 32 : 3 * LANES + 48, cols] = jnp.where(
                tail_keep, low[0:16], 0.0
            ).astype(jnp.bfloat16)
            toep[e, 3 * LANES + 48 : 4 * LANES, cols] = pad
        return 0

    loads[0].wait()
    loads[1].wait()
    fields = (img, var)
    last_cols = slice((BLOCKS - 1) * LANES, BLOCKS * LANES)

    def gather_edges(e, _):
        mine = (lane8 >= HALO * e) & (lane8 < HALO * (e + 1))
        for f in range(2):
            first = pltpu.roll(fields[f][e, :, 0:LANES], HALO * e, 1)
            last = pltpu.roll(fields[f][e, :, last_cols], (HALO * e + HALO) % LANES, 1)
            pack[0, f] = jnp.where(mine, first, pack[0, f])
            pack[1, f] = jnp.where(mine, last, pack[1, f])
        return 0

    lax.fori_loop(0, EPOCHS, gather_edges, 0)

    pl.semaphore_wait(barrier, 2 + len(offsets))
    halo_copies = []
    for side, target in ((0, left), (1, right)):
        copy = pltpu.make_async_remote_copy(
            src_ref=pack.at[side],
            dst_ref=halo.at[side],
            send_sem=halo_send.at[side],
            recv_sem=halo_recv.at[side],
            device_id=(me, target),
            device_id_type=MESH,
        )
        copy.start()
        halo_copies.append(copy)

    lax.fori_loop(0, EPOCHS, build, 0)

    def shifted(field, e, tile):
        def at(t):
            return pltpu.roll(field[e, :, t * LANES : (t + 1) * LANES], HALO, 1)

        f = 0 if field is img else 1
        if tile == 0:
            before = pltpu.roll(halo[1, f], (LANES - HALO * e) % LANES, 1) * jnp.where(
                sky == 0, 0.0, 1.0
            )
        else:
            before = at(tile - 1)
        if tile == BLOCKS:
            here = pltpu.roll(halo[0, f], (LANES + HALO - HALO * e) % LANES, 1) * jnp.where(
                sky == strips - 1, 0.0, 1.0
            )
        else:
            here = at(tile)
        return jnp.where(lane8 < HALO, before, here)

    def smear(blocks, e):
        left_rows = []
        for k in blocks:
            for field in fields:
                main_high, main_low = split(shifted(field, e, k))
                tail_high, tail_low = split(shifted(field, e, k + 1))
                tail_high = tail_high.astype(jnp.float32)
                tail = jnp.where(
                    lane8 < 16,
                    tail_high,
                    jnp.where(
                        lane8 < 32,
                        pltpu.roll(tail_low, 16, 1),
                        jnp.where(lane8 < 48, pltpu.roll(tail_high, 32, 1), 0.0),
                    ),
                )
                left_rows.append(
                    jnp.concatenate(
                        [main_high, main_low.astype(jnp.bfloat16), main_high, tail.astype(jnp.bfloat16)],
                        axis=1,
                    )
                )
        left_side = jnp.concatenate(left_rows, axis=0)
        spread = jnp.dot(left_side, toep[e], preferred_element_type=jnp.float32)
        spread_high, spread_low = split(spread)
        spread_low = spread_low.astype(jnp.bfloat16)
        count = 2 * len(blocks)

        def along(part, b):
            return jnp.concatenate(
                [part[i * ROWS : (i + 1) * ROWS, b * LANES : (b + 1) * LANES] for i in range(count)],
                axis=1,
            )

        total = None
        for b in range(BASES):
            high = along(spread_high, b)
            stacked = jnp.concatenate([high, along(spread_low, b), high], axis=0)
            smeared = jnp.dot(band[e, b][:, 0 : 3 * ROWS], stacked, preferred_element_type=jnp.float32)
            planes = []
            for k in blocks:
                plane = coef[e, b, :, k * LANES : (k + 1) * LANES].astype(jnp.float32)
                planes += [plane, plane]
            term = smeared * jnp.concatenate(planes, axis=1)
            total = term if total is None else total + term
        for i, k in enumerate(blocks):
            image = total[:, 2 * i * LANES : (2 * i + 1) * LANES]
            variance = total[:, (2 * i + 1) * LANES : (2 * i + 2) * LANES]
            weight = 1.0 / (variance + READ_NOISE)
            val[k, 0, e] = weight * image
            val[k, 1, e] = weight
        return 0

    def select(k, index, _):
        f, rows = index // (ROWS // 8), pl.ds(pl.multiple_of(index % (ROWS // 8) * 8, 8), 8)
        values = [val[k, f, e, rows, :] for e in range(EPOCHS)]
        sorts = [sort_four(values[i : i + 4]) for i in range(0, EPOCHS, 4)]
        pairs = []
        for i in (0, 2):
            pairs.append(
                (
                    sort_bitonic(lower_four(sorts[i], sorts[i + 1])),
                    sort_bitonic(upper_four(sorts[i], sorts[i + 1])),
                )
            )
        low, high = merge_ends(pairs[0], pairs[1])
        ends = low + high + [sum_tree(values)]
        for place, value in enumerate(ends):
            lists[k, f * (LISTS // 2) + place, rows, :] = value
        return 0

    def merge(pieces, last):
        result = []
        for f in range(2):
            base = f * (LISTS // 2)
            ends = []
            for piece in pieces:
                ends.append(
                    (
                        [piece(base + i) for i in range(REJECT)],
                        [piece(base + REJECT + i) for i in range(REJECT)],
                    )
                )
            low, high = merge_tree(ends)
            total = sum_tree([piece(base + 2 * REJECT) for piece in pieces])
            result.append((low, high, total))
        return result

    def first_axis(k):
        return k % 2

    def along_axis(axis, step):
        return peer_at(0, step) if axis == 0 else peer_at(step, 0)

    def place_on(axis, step):
        return (my_x + step) % SIDE if axis == 0 else (my_y + step) % SIDE

    def send_first(k):
        copies = []
        axis = first_axis(k)
        for step in range(1, SIDE):
            rows = pl.ds(pl.multiple_of(place_on(axis, step) * 8, 8), 8)
            copy = pltpu.make_async_remote_copy(
                src_ref=lists.at[k, :, rows, :],
                dst_ref=stage1.at[k, step - 1],
                send_sem=s1_send.at[k, step - 1],
                recv_sem=s1_recv.at[k, step - 1],
                device_id=(along_axis(axis, step), sky),
                device_id_type=MESH,
            )
            copy.start()
            copies.append(copy)
        return copies

    def send_second(k, copies):
        axis = first_axis(k)
        for copy in copies:
            copy.wait_recv()
        rows = pl.ds(pl.multiple_of(place_on(axis, 0) * 8, 8), 8)
        pieces = [lambda i: lists[k, i, rows, :]]
        for step in range(1, SIDE):
            pieces.append(lambda i, step=step: stage1[k, step - 1, i])
        for f, (low, high, total) in enumerate(merge(pieces, False)):
            for place, value in enumerate(low + high + [total]):
                mid[k, f * (LISTS // 2) + place] = value
        axis = 1 - axis
        own = pltpu.make_async_copy(
            mid.at[k, :, pl.ds(place_on(axis, 0) * 2, 2), :],
            stage2.at[0, :, pl.ds(2 * k, 2), :],
            own_sem.at[k],
        )
        own.start()
        result = []
        for step in range(1, SIDE):
            copy = pltpu.make_async_remote_copy(
                src_ref=mid.at[k, :, pl.ds(place_on(axis, step) * 2, 2), :],
                dst_ref=stage2.at[step, :, pl.ds(2 * k, 2), :],
                send_sem=s2_send.at[k, step - 1],
                recv_sem=s2_recv.at[k, step - 1],
                device_id=(along_axis(axis, step), sky),
                device_id_type=MESH,
            )
            copy.start()
            result.append(copy)
        return own, result

    firsts, seconds = {}, {}
    loads[2].wait()
    for number, blocks in enumerate(GROUPS):
        if number == 1:
            for copy in halo_copies:
                copy.wait_recv()
        lax.fori_loop(0, EPOCHS, lambda e, _: smear(blocks, e), 0)
        for k in blocks:
            lax.fori_loop(0, 2 * (ROWS // 8), lambda index, _: select(k, index, _), 0)
            firsts[k] = send_first(k)
    for blocks in GROUPS:
        for k in blocks:
            seconds[k] = send_second(k, firsts[k])
    for own, copies in seconds.values():
        own.wait()
        for copy in copies:
            copy.wait_recv()

    pieces = [lambda i, step=step: stage2[step, i] for step in range(SIDE)]
    for f, (low, high, total) in enumerate(merge(pieces, True)):
        final[me, f] = total - sum_tree(low) - sum_tree(high)
    copies = []
    for i, (dy, dx) in enumerate(offsets):
        copy = pltpu.make_async_remote_copy(
            src_ref=final.at[me],
            dst_ref=final.at[me],
            send_sem=fin_send.at[i],
            recv_sem=fin_recv.at[i],
            device_id=(peer_at(dy, dx), sky),
            device_id_type=MESH,
        )
        copy.start()
        copies.append(copy)
    for i, (dy, dx) in enumerate(offsets):
        source = peer_at(SIDE - dy, SIDE - dx)
        pltpu.make_async_remote_copy(
            src_ref=final.at[source],
            dst_ref=final.at[source],
            send_sem=fin_send.at[i],
            recv_sem=fin_recv.at[i],
            device_id=(source, sky),
            device_id_type=MESH,
        ).wait_recv()

    for k in range(BLOCKS):
        for outer in range(SIDE):
            for f in range(2):
                parts = []
                for inner in range(SIDE):
                    owner = inner * SIDE + outer if first_axis(k) == 0 else outer * SIDE + inner
                    parts.append(final[owner, f, 2 * k : 2 * k + 2, :])
                out_ref[f, outer * 8 : outer * 8 + 8, k * LANES : (k + 1) * LANES] = jnp.concatenate(
                    parts, axis=0
                )

    for copy in halo_copies:
        copy.wait_send()
    for k in range(BLOCKS):
        for copy in firsts[k] + seconds[k][1]:
            copy.wait_send()
    for copy in copies:
        copy.wait_send()


def per_device(images, variances, coefficients, row_filters, col_filters, dithers):
    f32, bf16 = jnp.float32, jnp.bfloat16
    dma = pltpu.SemaphoreType.DMA
    whole = pl.BlockSpec(memory_space=pltpu.VMEM)
    trimmed = pl.pallas_call(
        kernel,
        out_shape=jax.ShapeDtypeStruct((2, ROWS, BLOCKS * LANES), f32),
        in_specs=[pl.BlockSpec(memory_space=pl.ANY)] * 3
        + [whole, whole, pl.BlockSpec(memory_space=pltpu.SMEM)],
        out_specs=whole,
        scratch_shapes=[
            pltpu.VMEM((EPOCHS, ROWS, BLOCKS * LANES), f32),
            pltpu.VMEM((EPOCHS, ROWS, BLOCKS * LANES), f32),
            pltpu.VMEM((EPOCHS, BASES, ROWS, BLOCKS * LANES), bf16),
            pltpu.VMEM((2, EPOCHS * BASES, LANES), f32),
            pltpu.VMEM((4, EPOCHS * BASES * 8, LANES), f32),
            pltpu.VMEM((EPOCHS, 4 * LANES, BASES * LANES), bf16),
            pltpu.VMEM((EPOCHS, BASES, ROWS, LANES), bf16),
            pltpu.VMEM((2, 2, ROWS, LANES), f32),
            pltpu.VMEM((2, 2, ROWS, LANES), f32),
            pltpu.VMEM((BLOCKS, 2, EPOCHS, ROWS, LANES), f32),
            pltpu.VMEM((BLOCKS, LISTS, ROWS, LANES), f32),
            pltpu.VMEM((BLOCKS, SIDE - 1, LISTS, 8, LANES), f32),
            pltpu.VMEM((BLOCKS, LISTS, 8, LANES), f32),
            pltpu.VMEM((SIDE, LISTS, 8, LANES), f32),
            pltpu.VMEM((PEERS, 2, 8, LANES), f32),
            dma((3,)),
            dma((2,)),
            dma((2,)),
            dma((BLOCKS, SIDE - 1)),
            dma((BLOCKS, SIDE - 1)),
            dma((BLOCKS, SIDE - 1)),
            dma((BLOCKS, SIDE - 1)),
            dma((BLOCKS,)),
            dma((PEERS - 1,)),
            dma((PEERS - 1,)),
        ],
        compiler_params=pltpu.CompilerParams(
            collective_id=0, has_side_effects=True, vmem_limit_bytes=48 * 1024 * 1024
        ),
        name="coadd",
    )(images, variances, coefficients, row_filters, col_filters, dithers)
    kept_count = float(EPOCHS * lax.axis_size("epoch") - 2 * REJECT)
    return trimmed[0] / trimmed[1], trimmed[1] / kept_count


def solution(mesh):
    placed = (
        P("epoch", None, "sky"),
        P("epoch", None, "sky"),
        P("epoch", None, None, "sky"),
        P("epoch", None, None),
        P("epoch", None, None),
        P("epoch", None),
    )
    return jax.shard_map(
        per_device,
        mesh=mesh,
        in_specs=placed,
        out_specs=(P(None, "sky"), P(None, "sky")),
        check_vma=False,
    )
```

time: 475 us -> 53.3 us (0.11)
  waiting for transfers between devices: 195 us -> 0 us
  local copies, waits for them, and re-layouts: 139 us -> 6.46 us
  other arithmetic: 118 us -> 0.66 us
  Pallas kernels: 0 us -> 44.9 us
  between operations: 14.3 us -> 0.64 us
    all_gather x3 -> x0, waiting for transfers between devices: 195 us -> none  [combined_all(): pieces = jax.tree.map(lambda part: lax.all_gather(part, axis), value)]
    gather x48 -> x0, local copies, waits for them, and re-layouts: 70.3 us -> none
    pallas_call x0 -> x1, Pallas kernels: none -> 44.9 us  [per_device(): pl.pallas_call(kernel, out_shape=jax.ShapeDtypeStruct((2, ROWS, BLOCKS *...]
    max x77 -> x0, other arithmetic: 43.2 us -> none  [insert_high(): result[place] = jnp.maximum(slots[place], value)]
    slice x10 -> x0, local copies, waits for them, and re-layouts: 37.8 us -> none  [the longest x1 19.9 us: smear_all(): windows[:, :, None, 0:band_rows, :]]
    mul x24 -> x0, local copies, waits for them, and re-layouts: 30.9 us -> none  [the longest x10 13.2 us: smear_all(): row_taps[:, None, :, offset, None, None]]
    reduce_sum x4 -> x0, other arithmetic: 26.4 us -> none  [the longest x1 25.5 us: smear_all(): return jnp.sum(coeff_planes[:, None].astype(jnp.float32) * col_pass, axis=2)]
    min x30 -> x0, other arithmetic: 19.4 us -> none  [insert_low(): result.append(jnp.minimum(entry, value))]
  transfers between devices with their start and end apart: 5 -> 0, of which waited for: 3 -> 0; matrix products, arithmetic and copies ran while one was open for 11% -> 0% of each run, Pallas kernels for 0% -> 0%
where the time goes in v1:
time: 53.3 us; the launch traced here: 52.7 us
  Pallas kernels  44.9 us (84%)
  local copies, waits for them, and re-layouts  6.46 us (12%)
  other arithmetic  0.66 us (1%)
  between operations  0.64 us (1%)
    pallas_call x1, Pallas kernels, per_device(): pl.pallas_call(kernel, out_shape=jax.ShapeDtypeStruct((2, ROWS, BLOCKS *...  44.9 us
    unnamed x9, local copies, waits for them, and re-layouts  6.46 us

profile of v1, /device:TPU:2, one launch (start us, length us, event | category | flops | bytes accessed | tf_op | source)
XLA Modules:
  0.0 52.7 jit_solution(6099296838956016497)
XLA Ops:
  0.6 0.8 %copy.10.dith_ref = s32[16,2]{1,0:T(8,128)S(1)} copy(s32[16,2]{0,1:T(2,128)} %param.11) | data formatting | bytes 256 | tf_op args[5]
  1.4 0.8 %copy.8.rowf_ref = f32[16,4,11]{2,1,0:T(4,128)S(1)} copy(f32[16,4,11]{0,1,2:T(4,128)} %param.9) | data formatting | bytes 5632 | tf_op args[3]
  2.2 0.8 %copy.9.colf_ref = f32[16,4,11]{2,1,0:T(4,128)S(1)} copy(f32[16,4,11]{0,1,2:T(4,128)} %param.10) | data formatting | bytes 5632 | tf_op args[4]
  3.0 0.0 copy-start
  3.1 1.6 %copy-done = bf16[16,4,32,512]{3,2,1,0:T(8,128)(2,1)S(1)} copy-done((bf16[16,4,32,512]{3,2,1,0:T(8,128)(2,1)S(1)}, bf16[16,4,32,512]{3,2,1,0:T(8,128)(2,1)}, u32[]{:S(2)}) %copy-start) | copy-done | bytes 2097176
  4.6 0.0 copy-start.1
  4.6 1.2 %copy-done.1 = f32[16,32,512]{2,1,0:T(8,128)S(1)} copy-done((f32[16,32,512]{2,1,0:T(8,128)S(1)}, f32[16,32,512]{2,1,0:T(8,128)}, u32[]{:S(2)}) %copy-start.1) | copy-done | bytes 1048600
  5.9 0.0 copy-start.2
  5.9 1.2 %copy-done.2 = f32[16,32,512]{2,1,0:T(8,128)S(1)} copy-done((f32[16,32,512]{2,1,0:T(8,128)S(1)}, f32[16,32,512]{2,1,0:T(8,128)}, u32[]{:S(2)}) %copy-start.2) | copy-done | bytes 1048600
  7.1 44.9 %coadd.1 = f32[2,32,512]{2,1,0:T(8,128)S(1)} custom-call(f32[16,32,512]{2,1,0:T(8,128)S(1)} %copy-done.1, f32[16,32,512]{2,1,0:T(8,128)S(1)} %copy-done.2, bf16[16,4,32,512]{3,2,1,0:T(8,128)(2,1)S(1)} %copy-done, f32[16,4,11]{2,1,0:T(4,128)S(1)} %copy.8.rowf_ref, f32[16,4,11]{2,1,0:T(4,128)S(1)} %copy.9.colf_ref, s32[16,2]{1,0:T(8,128)S(1)} %copy.10.dith_ref), custom_call_target="tpu_custom_call" | custom-call | tf_op jit(solution)/shard_map/coadd/pallas_call | solution.py:439
  52.0 0.7 %multiply_bitcast_fusion = (f32[32,512]{1,0:T(8,128)}, f32[32,512]{1,0:T(8,128)}) fusion(f32[2,32,512]{2,1,0:T(8,128)S(1)} %coadd.1), kind=kLoop, calls=%fused_computation | loop fusion | flops 32768 | bytes 262144 | tf_op jit(solution)/shard_map/div | solution.py:478
Async XLA Ops:
  3.0 1.6 %copy-start = (bf16[16,4,32,512]{3,2,1,0:T(8,128)(2,1)S(1)}, bf16[16,4,32,512]{3,2,1,0:T(8,128)(2,1)}, u32[]{:S(2)}) copy-start(bf16[16,4,32,512]{3,2,1,0:T(8,128)(2,1)} %coef_hbm.1) | copy-start | bytes 6291460
  4.6 1.2 %copy-start.1 = (f32[16,32,512]{2,1,0:T(8,128)S(1)}, f32[16,32,512]{2,1,0:T(8,128)}, u32[]{:S(2)}) copy-start(f32[16,32,512]{2,1,0:T(8,128)} %img_hbm.1) | copy-start | bytes 3145732
  5.9 1.2 %copy-start.2 = (f32[16,32,512]{2,1,0:T(8,128)S(1)}, f32[16,32,512]{2,1,0:T(8,128)}, u32[]{:S(2)}) copy-start(f32[16,32,512]{2,1,0:T(8,128)} %var_hbm.1) | copy-start | bytes 3145732

commit v2 on v0

v2 whole, which is shorter than its diff:
```python
import jax
import jax.numpy as jnp
from jax import lax
from jax.experimental import pallas as pl
from jax.experimental.pallas import tpu as pltpu
from jax.sharding import PartitionSpec as P

TAPS = 11
BASES = 4
REJECT = 4
HALF = 5
HALO = 8
READ_NOISE = 0.25

LANES = 128
EPOCHS = 16
ROWS = 32
BLOCKS = 4
SIDE = 4
PEERS = SIDE * SIDE
LISTS = 2 * REJECT + 1
HALVES = ((1, 2), (0, 3))
OWNER_ROWS = 8
MESH = pl.DeviceIdType.MESH


def split(value):
    high = value.astype(jnp.bfloat16)
    return high, value - high.astype(jnp.float32)


def exchange(first, second):
    return jnp.minimum(first, second), jnp.maximum(first, second)


def sort_four(values):
    a, b, c, d = values
    a, b = exchange(a, b)
    c, d = exchange(c, d)
    a, c = exchange(a, c)
    b, d = exchange(b, d)
    b, c = exchange(b, c)
    return [a, b, c, d]


def sort_bitonic(values):
    a, b, c, d = values
    a, c = exchange(a, c)
    b, d = exchange(b, d)
    a, b = exchange(a, b)
    c, d = exchange(c, d)
    return [a, b, c, d]


def lower_four(first, second):
    return [jnp.minimum(first[i], second[REJECT - 1 - i]) for i in range(REJECT)]


def upper_four(first, second):
    return [jnp.maximum(first[i], second[REJECT - 1 - i]) for i in range(REJECT)]


def merge_ends(first, second, last=False):
    low = lower_four(first[0], second[0])
    high = upper_four(first[1], second[1])
    if not last:
        low, high = sort_bitonic(low), sort_bitonic(high)
    return low, high


def sum_tree(values):
    values = list(values)
    while len(values) > 1:
        values = [values[i] + values[i + 1] for i in range(0, len(values) - 1, 2)] + (
            [values[-1]] if len(values) % 2 else []
        )
    return values[0]


def kernel(
    img_hbm, var_hbm, coef_hbm, rowf_hbm, colf_hbm, dith_hbm, out_ref,
    img, var, coef, rowf, colf, dith, filt, base, spread_high, spread_low, spread_tail, band, ext_high, ext_low, ext_tail,
    spread_high1, spread_low1, spread_tail1, band1, ext_high1, ext_low1, ext_tail1, pack, halo, edge, col0, col1, val, lists,
    near_low, near_high, mid_low, mid_high, far_low, far_high, final,
    in_sem, halo_send, halo_recv, near_send, near_recv, far_send, far_recv, fin_send, fin_recv,
):
    f32, bf16 = jnp.float32, jnp.bfloat16
    pairs = (
        (spread_high, spread_low, spread_tail, band, ext_high, ext_low, ext_tail),
        (spread_high1, spread_low1, spread_tail1, band1, ext_high1, ext_low1, ext_tail1),
    )
    me = lax.axis_index("epoch")
    sky = lax.axis_index("sky")
    strips = lax.axis_size("sky")
    my_y, my_x = me // SIDE, me % SIDE
    right, left = (sky + 1) % strips, (sky + strips - 1) % strips

    def peer_at(dy, dx):
        return ((my_y + dy) % SIDE) * SIDE + (my_x + dx) % SIDE

    offsets = [(dy, dx) for dy in range(SIDE) for dx in range(SIDE) if dy or dx]

    loads = [
        pltpu.make_async_copy(source, target, in_sem.at[i])
        for i, (source, target) in enumerate(
            (
                (rowf_hbm, rowf),
                (colf_hbm, colf),
                (dith_hbm, dith),
                (img_hbm, img),
                (var_hbm, var),
                (coef_hbm, coef),
            )
        )
    ]
    for load in loads:
        load.start()

    barrier = pltpu.get_barrier_semaphore()
    for neighbour in (left, right):
        pl.semaphore_signal(barrier, inc=1, device_id=(me, neighbour), device_id_type=MESH)
    for dy, dx in offsets:
        pl.semaphore_signal(barrier, inc=1, device_id=(peer_at(dy, dx), sky), device_id_type=MESH)

    lane = lax.broadcasted_iota(jnp.int32, (ROWS, LANES), 1)
    lane16 = lane[0:16]

    def within(start, stop, like=lane):
        return jnp.where((like >= start) & (like < stop), 1.0, 0.0).astype(bf16)

    filt[...] = jnp.zeros_like(filt)
    loads[0].wait()
    loads[1].wait()
    for j in range(TAPS):
        for b in range(BASES):
            filt[16 * b + j, 0:EPOCHS] = rowf[j, b, :]
            filt[64 + 16 * b + TAPS - 1 - j, 0:EPOCHS] = colf[j, b, :]
    turned = jnp.transpose(filt[...])[0:EPOCHS]
    for kind in range(2):
        for b in range(BASES):
            at = 16 * (BASES * kind + b)
            taps = pltpu.roll(turned, LANES - at, 1) if at else turned
            taps = jnp.where(lane16 < 16, taps, 0.0)
            high, low = split(taps)
            for part, value in enumerate((high.astype(f32), low.astype(bf16).astype(f32))):
                for turn in range(8):
                    rows = pl.ds(b * EPOCHS * 8 + turn, EPOCHS, stride=8)
                    base[2 * kind + part, rows, :] = pltpu.roll(value, turn, 1) if turn else value

    loads[3].wait()
    loads[4].wait()
    fields = (img, var)
    last_cols = slice((BLOCKS - 1) * LANES, BLOCKS * LANES)

    def gather_edges(e, _):
        mine = (lane >= HALO * e) & (lane < HALO * (e + 1))
        for f in range(2):
            first = pltpu.roll(fields[f][e, :, 0:LANES], HALO * e, 1)
            last = pltpu.roll(fields[f][e, :, last_cols], (HALO * e + HALO) % LANES, 1)
            pack[0, f] = jnp.where(mine, first, pack[0, f])
            pack[1, f] = jnp.where(mine, last, pack[1, f])
        return 0

    lax.fori_loop(0, EPOCHS, gather_edges, 0, unroll=4)

    pl.semaphore_wait(barrier, 2 + len(offsets))
    halo_copies = []
    for side, target in ((0, left), (1, right)):
        copy = pltpu.make_async_remote_copy(
            src_ref=pack.at[side],
            dst_ref=halo.at[side],
            send_sem=halo_send.at[side],
            recv_sem=halo_recv.at[side],
            device_id=(me, target),
            device_id_type=MESH,
        )
        copy.start()
        halo_copies.append(copy)

    loads[2].wait()

    def build(parity, n):
        spread_high, spread_low, spread_tail, band = pairs[parity][0:4]
        e = 2 * n + parity
        row_turn, col_turn = 8 - dith[0, e], dith[1, e]
        for b in range(BASES):
            at = pl.ds(pl.multiple_of((b * EPOCHS + e) * 8, 8), 8)

            def sixteen(which):
                eight = base[which, at, :]
                return jnp.concatenate([eight, pltpu.roll(eight, 8, 1)], axis=0).astype(bf16)

            high, low = sixteen(0), sixteen(1)
            for g in range(2):
                turn = row_turn + (16 * g - HALF - 8) % LANES
                main = pltpu.roll(high, turn, 1) * within(0, ROWS, lane16)
                rest = pltpu.roll(low, turn, 1) * within(0, ROWS, lane16)
                band[n, b, 16 * g : 16 * g + 16, :] = (
                    main + pltpu.roll(main, ROWS, 1) + pltpu.roll(rest, 2 * ROWS, 1)
                )
            tails = []
            for which, target in ((2, spread_high), (3, spread_low)):
                taps = sixteen(which)
                for g in range(8):
                    value = pltpu.roll(taps, col_turn + (16 * g - 13) % LANES, 1)
                    if g == 0:
                        tails.append(value * within(64, LANES, lane16))
                        value = value * within(0, 64, lane16)
                    target[n, b, 16 * g : 16 * g + 16, :] = value
            spread_tail[n, b] = jnp.concatenate([tails[0], tails[0], tails[1]], axis=0)

    def extend(parity, n):
        ext_high, ext_low, ext_tail = pairs[parity][4:7]
        e = 2 * n + parity
        for f in range(2):
            highs, lows = [], []
            for t in range(BLOCKS):
                high, low = split(fields[f][e, :, t * LANES : (t + 1) * LANES])
                highs.append(pltpu.roll(high, HALO, 1))
                lows.append(pltpu.roll(low.astype(bf16), HALO, 1))

            def tile(parts, t):
                value = 0
                if t > 0:
                    value = parts[t - 1] * within(0, HALO)
                if t < BLOCKS:
                    value = value + parts[t] * within(HALO, LANES)
                return value

            highs = [tile(highs, t) for t in range(BLOCKS + 1)]
            lows = [tile(lows, t) for t in range(BLOCKS + 1)]
            for t in range(BLOCKS):
                ext_high[n, f, t] = highs[t]
                ext_low[n, f, t] = lows[t]
                ext_tail[n, f, t] = (
                    highs[t + 1] * within(0, 16)
                    + pltpu.roll(lows[t + 1], 16, 1) * within(16, 32)
                    + pltpu.roll(highs[t + 1], 32, 1) * within(32, 48)
                )

    def spread(half, parity, n, target):
        spread_high, spread_low, spread_tail, _, ext_high, ext_low, ext_tail = pairs[parity]
        e = 2 * n + parity
        highs, lows, tails = [], [], []
        for f in range(2):
            for k in HALVES[half]:
                high, low, tail = ext_high[n, f, k], ext_low[n, f, k], ext_tail[n, f, k]
                if k == 0:
                    turn = (LANES - HALO * e) % LANES
                    high = high + pltpu.roll(edge[0, 0, f], turn, 1) * within(0, HALO)
                    low = low + pltpu.roll(edge[0, 1, f], turn, 1) * within(0, HALO)
                if k == BLOCKS - 1:
                    for part, to in ((0, 8), (1, 24), (0, 40)):
                        turn = (LANES + to - HALO * e) % LANES
                        tail = tail + pltpu.roll(edge[1, part, f], turn, 1) * within(to, to + HALO)
                highs.append(high)
                lows.append(low)
                tails.append(tail)
        highs, lows, tails = (jnp.concatenate(parts, axis=0) for parts in (highs, lows, tails))
        data = jnp.concatenate([highs, lows, highs, tails], axis=1)
        cols = []
        for b in range(BASES):
            high = spread_high[n, b]
            cols.append(jnp.concatenate([high, high, spread_low[n, b], spread_tail[n, b]], axis=0))
        taps = jnp.concatenate(cols, axis=1)
        result = jnp.dot(data[:, 0 : taps.shape[0]], taps, preferred_element_type=f32)
        high, low = split(result)
        low = low.astype(bf16)
        for b in range(BASES):
            for i in range(4):
                rows, lanes = slice(i * ROWS, (i + 1) * ROWS), slice(b * LANES, (b + 1) * LANES)
                target[0, b, i] = high[rows, lanes]
                target[1, b, i] = low[rows, lanes]

    def finish(half, parity, n, source):
        band = pairs[parity][3]
        e = 2 * n + parity
        total = [None] * 4
        for b in range(BASES):
            high = jnp.concatenate([source[0, b, i] for i in range(4)], axis=1)
            low = jnp.concatenate([source[1, b, i] for i in range(4)], axis=1)
            smeared = jnp.dot(
                band[n, b][:, 0 : 3 * ROWS],
                jnp.concatenate([high, low, high], axis=0),
                preferred_element_type=f32,
            )
            for i in range(4):
                k = HALVES[half][i % 2]
                plane = coef[e, b, :, k * LANES : (k + 1) * LANES].astype(f32)
                term = smeared[:, i * LANES : (i + 1) * LANES] * plane
                total[i] = term if total[i] is None else total[i] + term
        for i in range(2):
            weight = 1.0 / (total[2 + i] + READ_NOISE)
            val[half, e, 0, i] = weight * total[i]
            val[half, e, 1, i] = weight

    def smear(half):
        def prepare(parity, n):
            if half == 0:
                build(parity, n)
                extend(parity, n)

        def step(n, _):
            later = (n + 1) % (EPOCHS // 2)
            spread(half, 1, n, col1)
            prepare(0, later)
            finish(half, 0, n, col0)
            spread(half, 0, later, col0)
            prepare(1, later)
            finish(half, 1, n, col1)
            return 0

        prepare(0, 0)
        prepare(1, 0)
        spread(half, 0, 0, col0)
        lax.fori_loop(0, EPOCHS // 2, step, 0)

    def select(half, index, _):
        f, i = index // (2 * SIDE), index // SIDE % 2
        rows = pl.ds(pl.multiple_of(index % SIDE * 8, 8), 8)
        values = [val[half, e, f, i, rows, :] for e in range(EPOCHS)]
        sorts = [sort_four(values[i : i + 4]) for i in range(0, EPOCHS, 4)]
        pairs = []
        for i in (0, 2):
            pairs.append(
                (
                    sort_bitonic(lower_four(sorts[i], sorts[i + 1])),
                    sort_bitonic(upper_four(sorts[i], sorts[i + 1])),
                )
            )
        low, high = merge_ends(pairs[0], pairs[1])
        for place, value in enumerate(low + high + [sum_tree(values)]):
            lists[half, place, index // SIDE, index % SIDE] = value
        return 0

    def copy_to(source, target, send, receive, dy, dx):
        copy = pltpu.make_async_remote_copy(
            src_ref=source,
            dst_ref=target,
            send_sem=send,
            recv_sem=receive,
            device_id=(peer_at(dy, dx), sky),
            device_id_type=MESH,
        )
        copy.start()
        return copy

    def send_near(half):
        copies = []
        for step in (2, 1, 3):
            x, y = (my_x + step) % SIDE, (my_y + step) % SIDE
            sems = [(near_send.at[half, i, step - 1], near_recv.at[half, i, step - 1]) for i in range(2)]
            low = copy_to(
                lists.at[half, pl.ds(0, REJECT), x], near_low.at[half, step - 1], *sems[0], 0, step
            )
            high = copy_to(
                lists.at[half, pl.ds(REJECT, REJECT + 1), :, y],
                near_high.at[half, step - 1],
                *sems[1],
                step,
                0,
            )
            copies += [low, high]
        return copies

    def tree(parts, pick):
        while len(parts) > 1:
            parts = [sort_bitonic(pick(parts[i], parts[i + 1])) for i in range(0, len(parts), 2)]
        return parts[0]

    def send_far(half, copies):
        for copy in copies:
            copy.wait_recv()
        for g in range(SIDE):
            parts = [[lists[half, i, my_x, g] for i in range(REJECT)]]
            for step in range(SIDE - 1):
                parts.append([near_low[half, step, i, g] for i in range(REJECT)])
            for i, value in enumerate(tree(parts, lower_four)):
                mid_low[half, i, g] = value
            parts = [[lists[half, REJECT + i, g, my_y] for i in range(REJECT + 1)]]
            for step in range(SIDE - 1):
                parts.append([near_high[half, step, i, g] for i in range(REJECT + 1)])
            for i, value in enumerate(tree([part[0:REJECT] for part in parts], upper_four)):
                mid_high[half, i, g] = value
            mid_high[half, REJECT, g] = sum_tree([part[REJECT] for part in parts])
        result = []
        for step in (2, 1, 3):
            x, y = (my_x + step) % SIDE, (my_y + step) % SIDE
            sems = [(far_send.at[half, i, step - 1], far_recv.at[half, i, step - 1]) for i in range(2)]
            low = copy_to(mid_low.at[half, :, y], far_low.at[half, step - 1], *sems[0], step, 0)
            high = copy_to(mid_high.at[half, :, x], far_high.at[half, step - 1], *sems[1], 0, step)
            result += [low, high]
        return result

    def close(half, copies):
        for copy in copies:
            copy.wait_recv()
        lows = [[mid_low[half, i, my_y] for i in range(REJECT)]]
        highs = [[mid_high[half, i, my_x] for i in range(REJECT + 1)]]
        for step in range(SIDE - 1):
            lows.append([far_low[half, step, i] for i in range(REJECT)])
            highs.append([far_high[half, step, i] for i in range(REJECT + 1)])
        low = lower_four(*(sort_bitonic(lower_four(lows[i], lows[i + 1])) for i in (0, 2)))
        high = upper_four(*(sort_bitonic(upper_four(highs[i], highs[i + 1])) for i in (0, 2)))
        total = sum_tree([part[REJECT] for part in highs])
        final[me, half] = total - sum_tree(low) - sum_tree(high)

    loads[5].wait()
    smear(0)
    lax.fori_loop(0, PEERS, lambda index, _: select(0, index, _), 0, unroll=2)
    near0 = send_near(0)
    for copy in halo_copies:
        copy.wait_recv()
    for side, at_end in ((0, 0), (1, strips - 1)):
        for f in range(2):
            value = halo[1 - side, f] * jnp.where(sky == at_end, 0.0, 1.0)
            high, low = split(value)
            edge[side, 0, f] = high
            edge[side, 1, f] = low.astype(bf16)
    smear(1)
    lax.fori_loop(0, PEERS, lambda index, _: select(1, index, _), 0, unroll=2)
    near1 = send_near(1)
    far0 = send_far(0, near0)
    far1 = send_far(1, near1)
    close(0, far0)
    close(1, far1)

    copies = [
        copy_to(final.at[me], final.at[me], fin_send.at[i], fin_recv.at[i], dy, dx)
        for i, (dy, dx) in enumerate(offsets)
    ]
    for i, (dy, dx) in enumerate(offsets):
        source = peer_at(SIDE - dy, SIDE - dx)
        pltpu.make_async_remote_copy(
            src_ref=final.at[source],
            dst_ref=final.at[source],
            send_sem=fin_send.at[i],
            recv_sem=fin_recv.at[i],
            device_id=(source, sky),
            device_id_type=MESH,
        ).wait_recv()

    for half, blocks in enumerate(HALVES):
        for unit in range(PEERS):
            f, k, g = unit // (2 * SIDE), blocks[unit // SIDE % 2], unit % SIDE
            out_ref[f, 8 * g : 8 * g + 8, k * LANES : (k + 1) * LANES] = final[
                (unit % SIDE) * SIDE + unit // SIDE, half
            ]

    for copy in halo_copies + near0 + near1 + far0 + far1 + copies:
        copy.wait_send()


def per_device(images, variances, coefficients, row_filters, col_filters, dithers):
    f32, bf16 = jnp.float32, jnp.bfloat16
    dma, vmem = pltpu.SemaphoreType.DMA, pltpu.VMEM
    tile = (OWNER_ROWS, LANES)
    trimmed = pl.pallas_call(
        kernel,
        out_shape=jax.ShapeDtypeStruct((2, ROWS, BLOCKS * LANES), f32),
        in_specs=[pl.BlockSpec(memory_space=pl.ANY)] * 6,
        out_specs=pl.BlockSpec(memory_space=pltpu.VMEM),
        scratch_shapes=[
            vmem((EPOCHS, ROWS, BLOCKS * LANES), f32),
            vmem((EPOCHS, ROWS, BLOCKS * LANES), f32),
            vmem((EPOCHS, BASES, ROWS, BLOCKS * LANES), bf16),
            vmem((TAPS, BASES, EPOCHS), f32),
            vmem((TAPS, BASES, EPOCHS), f32),
            pltpu.SMEM((2, EPOCHS), jnp.int32),
            vmem((LANES, LANES), f32),
            vmem((4, EPOCHS * BASES * 8, LANES), f32),
            *(
                2
                * [
                vmem((EPOCHS // 2, BASES, LANES, LANES), bf16),
                vmem((EPOCHS // 2, BASES, LANES, LANES), bf16),
                vmem((EPOCHS // 2, BASES, 48, LANES), bf16),
                vmem((EPOCHS // 2, BASES, ROWS, LANES), bf16),
                vmem((EPOCHS // 2, 2, BLOCKS, ROWS, LANES), bf16),
                vmem((EPOCHS // 2, 2, BLOCKS, ROWS, LANES), bf16),
                vmem((EPOCHS // 2, 2, BLOCKS, ROWS, LANES), bf16),
                ]
            ),
            vmem((2, 2, ROWS, LANES), f32),
            vmem((2, 2, ROWS, LANES), f32),
            vmem((2, 2, 2, ROWS, LANES), bf16),
            vmem((2, BASES, 4, ROWS, LANES), bf16),
            vmem((2, BASES, 4, ROWS, LANES), bf16),
            vmem((2, EPOCHS, 2, 2, ROWS, LANES), f32),
            vmem((2, LISTS, SIDE, SIDE) + tile, f32),
            vmem((2, SIDE - 1, REJECT, SIDE) + tile, f32),
            vmem((2, SIDE - 1, REJECT + 1, SIDE) + tile, f32),
            vmem((2, REJECT, SIDE) + tile, f32),
            vmem((2, REJECT + 1, SIDE) + tile, f32),
            vmem((2, SIDE - 1, REJECT) + tile, f32),
            vmem((2, SIDE - 1, REJECT + 1) + tile, f32),
            vmem((PEERS, 2) + tile, f32),
            dma((6,)),
            dma((2,)),
            dma((2,)),
            dma((2, 2, SIDE - 1)),
            dma((2, 2, SIDE - 1)),
            dma((2, 2, SIDE - 1)),
            dma((2, 2, SIDE - 1)),
            dma((PEERS - 1,)),
            dma((PEERS - 1,)),
        ],
        compiler_params=pltpu.CompilerParams(
            collective_id=0, has_side_effects=True, vmem_limit_bytes=66_000_000
        ),
        name="coadd",
    )(
        images,
        variances,
        coefficients,
        jnp.transpose(row_filters, (2, 1, 0)),
        jnp.transpose(col_filters, (2, 1, 0)),
        jnp.transpose(dithers),
    )
    kept_count = float(EPOCHS * lax.axis_size("epoch") - 2 * REJECT)
    return trimmed[0] / trimmed[1], trimmed[1] / kept_count


def solution(mesh):
    placed = (
        P("epoch", None, "sky"),
        P("epoch", None, "sky"),
        P("epoch", None, None, "sky"),
        P("epoch", None, None),
        P("epoch", None, None),
        P("epoch", None),
    )
    return jax.shard_map(
        per_device,
        mesh=mesh,
        in_specs=placed,
        out_specs=(P(None, "sky"), P(None, "sky")),
        check_vma=False,
    )
```

time: 475 us -> 39.9 us (0.08)
  waiting for transfers between devices: 195 us -> 0 us
  local copies, waits for them, and re-layouts: 139 us -> 0 us
  other arithmetic: 118 us -> 1.53 us
  Pallas kernels: 0 us -> 37.6 us
  between operations: 14.3 us -> 0.64 us
    all_gather x3 -> x0, waiting for transfers between devices: 195 us -> none  [combined_all(): pieces = jax.tree.map(lambda part: lax.all_gather(part, axis), value)]
    gather x48 -> x0, local copies, waits for them, and re-layouts: 70.3 us -> none
    max x77 -> x0, other arithmetic: 43.2 us -> none  [insert_high(): result[place] = jnp.maximum(slots[place], value)]
    slice x10 -> x0, local copies, waits for them, and re-layouts: 37.8 us -> none  [the longest x1 19.9 us: smear_all(): windows[:, :, None, 0:band_rows, :]]
    pallas_call x0 -> x1, Pallas kernels: none -> 37.6 us  [per_device(): pl.pallas_call(kernel, out_shape=jax.ShapeDtypeStruct((2, ROWS, BLOCKS *...]
    mul x24 -> x0, local copies, waits for them, and re-layouts: 30.9 us -> none  [the longest x10 13.2 us: smear_all(): row_taps[:, None, :, offset, None, None]]
    reduce_sum x4 -> x0, other arithmetic: 26.4 us -> none  [the longest x1 25.5 us: smear_all(): return jnp.sum(coeff_planes[:, None].astype(jnp.float32) * col_pass, axis=2)]
    min x30 -> x0, other arithmetic: 19.4 us -> none  [insert_low(): result.append(jnp.minimum(entry, value))]
  transfers between devices with their start and end apart: 5 -> 0, of which waited for: 3 -> 0; matrix products, arithmetic and copies ran while one was open for 11% -> 0% of each run, Pallas kernels for 0% -> 0%
where the time goes in v2:
time: 39.9 us; the launch traced here: 39.8 us
  Pallas kernels  37.6 us (94%)
  other arithmetic  1.53 us (4%)
  between operations  0.64 us (2%)
    pallas_call x1, Pallas kernels, per_device(): pl.pallas_call(kernel, out_shape=jax.ShapeDtypeStruct((2, ROWS, BLOCKS *...  37.6 us
    div x1, other arithmetic, per_device(): return (trimmed[0] / trimmed[1], trimmed[1] / kept_count)  1.53 us

profile of v2, /device:TPU:2, one launch (start us, length us, event | category | flops | bytes accessed | tf_op | source)
XLA Modules:
  0.0 39.8 jit_solution(17659732971505026698)
XLA Ops:
  0.6 37.6 %coadd.1 = f32[2,32,512]{2,1,0:T(8,128)} custom-call(f32[16,32,512]{2,1,0:T(8,128)} %img_hbm.1, f32[16,32,512]{2,1,0:T(8,128)} %var_hbm.1, bf16[16,4,32,512]{3,2,1,0:T(8,128)(2,1)} %coef_hbm.1, f32[11,4,16]{2,1,0:T(4,128)} %bitcast.7, f32[11,4,16]{2,1,0:T(4,128)} %bitcast.8, s32[2,16]{1,0:T(2,128)} %bitcast.9), custom_call_target="tpu_custom_call" | custom-call | tf_op jit(solution)/shard_map/coadd/pallas_call | solution.py:458
  38.2 1.5 %multiply_bitcast_fusion = (f32[32,512]{1,0:T(8,128)}, f32[32,512]{1,0:T(8,128)}) fusion(f32[2,32,512]{2,1,0:T(8,128)} %coadd.1), kind=kLoop, calls=%fused_computation | loop fusion | flops 32768 | bytes 262144 | tf_op jit(solution)/shard_map/div | solution.py:521

commit v3 on v2

--- a/solution.py
+++ b/solution.py
@@ -79,16 +79,11 @@
 
 def kernel(
     img_hbm, var_hbm, coef_hbm, rowf_hbm, colf_hbm, dith_hbm, out_ref,
-    img, var, coef, rowf, colf, dith, filt, base, spread_high, spread_low, spread_tail, band, ext_high, ext_low, ext_tail,
-    spread_high1, spread_low1, spread_tail1, band1, ext_high1, ext_low1, ext_tail1, pack, halo, edge, col0, col1, val, lists,
+    img, var, coef, rowf, colf, dith, filt, base, pack, halo, edge, col0, col1, val, lists,
     near_low, near_high, mid_low, mid_high, far_low, far_high, final,
     in_sem, halo_send, halo_recv, near_send, near_recv, far_send, far_recv, fin_send, fin_recv,
 ):
     f32, bf16 = jnp.float32, jnp.bfloat16
-    pairs = (
-        (spread_high, spread_low, spread_tail, band, ext_high, ext_low, ext_tail),
-        (spread_high1, spread_low1, spread_tail1, band1, ext_high1, ext_low1, ext_tail1),
-    )
     me = lax.axis_index("epoch")
     sky = lax.axis_index("sky")
     strips = lax.axis_size("sky")
@@ -98,7 +93,8 @@
     def peer_at(dy, dx):
         return ((my_y + dy) % SIDE) * SIDE + (my_x + dx) % SIDE
 
-    offsets = [(dy, dx) for dy in range(SIDE) for dx in range(SIDE) if dy or dx]
+    offsets = [(dy, dx) for dy in (2, 1, 3, 0) for dx in (2, 1, 3, 0) if dy or dx]
+    offsets.sort(key=lambda o: -(2 - abs(2 - o[0]) + 2 - abs(2 - o[1])))
 
     loads = [
         pltpu.make_async_copy(source, target, in_sem.at[i])
@@ -142,10 +138,12 @@
             taps = pltpu.roll(turned, LANES - at, 1) if at else turned
             taps = jnp.where(lane16 < 16, taps, 0.0)
             high, low = split(taps)
-            for part, value in enumerate((high.astype(f32), low.astype(bf16).astype(f32))):
-                for turn in range(8):
-                    rows = pl.ds(b * EPOCHS * 8 + turn, EPOCHS, stride=8)
-                    base[2 * kind + part, rows, :] = pltpu.roll(value, turn, 1) if turn else value
+            high, low = high.astype(f32), low.astype(bf16).astype(f32)
+            if kind == 0:
+                parts = high + pltpu.roll(high, ROWS, 1) + pltpu.roll(low, 2 * ROWS, 1)
+            else:
+                parts = high + pltpu.roll(low, 64, 1)
+            base[kind, b * EPOCHS : (b + 1) * EPOCHS, :] = parts
 
     loads[3].wait()
     loads[4].wait()
@@ -163,106 +161,69 @@
 
     lax.fori_loop(0, EPOCHS, gather_edges, 0, unroll=4)
 
-    pl.semaphore_wait(barrier, 2 + len(offsets))
-    halo_copies = []
-    for side, target in ((0, left), (1, right)):
-        copy = pltpu.make_async_remote_copy(
-            src_ref=pack.at[side],
-            dst_ref=halo.at[side],
-            send_sem=halo_send.at[side],
-            recv_sem=halo_recv.at[side],
-            device_id=(me, target),
-            device_id_type=MESH,
-        )
-        copy.start()
-        halo_copies.append(copy)
-
     loads[2].wait()
 
-    def build(parity, n):
-        spread_high, spread_low, spread_tail, band = pairs[parity][0:4]
-        e = 2 * n + parity
-        row_turn, col_turn = 8 - dith[0, e], dith[1, e]
-        for b in range(BASES):
-            at = pl.ds(pl.multiple_of((b * EPOCHS + e) * 8, 8), 8)
-
-            def sixteen(which):
-                eight = base[which, at, :]
-                return jnp.concatenate([eight, pltpu.roll(eight, 8, 1)], axis=0).astype(bf16)
-
-            high, low = sixteen(0), sixteen(1)
-            for g in range(2):
-                turn = row_turn + (16 * g - HALF - 8) % LANES
-                main = pltpu.roll(high, turn, 1) * within(0, ROWS, lane16)
-                rest = pltpu.roll(low, turn, 1) * within(0, ROWS, lane16)
-                band[n, b, 16 * g : 16 * g + 16, :] = (
-                    main + pltpu.roll(main, ROWS, 1) + pltpu.roll(rest, 2 * ROWS, 1)
-                )
-            tails = []
-            for which, target in ((2, spread_high), (3, spread_low)):
-                taps = sixteen(which)
-                for g in range(8):
-                    value = pltpu.roll(taps, col_turn + (16 * g - 13) % LANES, 1)
-                    if g == 0:
-                        tails.append(value * within(64, LANES, lane16))
-                        value = value * within(0, 64, lane16)
-                    target[n, b, 16 * g : 16 * g + 16, :] = value
-            spread_tail[n, b] = jnp.concatenate([tails[0], tails[0], tails[1]], axis=0)
-
-    def extend(parity, n):
-        ext_high, ext_low, ext_tail = pairs[parity][4:7]
-        e = 2 * n + parity
-        for f in range(2):
-            highs, lows = [], []
-            for t in range(BLOCKS):
-                high, low = split(fields[f][e, :, t * LANES : (t + 1) * LANES])
-                highs.append(pltpu.roll(high, HALO, 1))
-                lows.append(pltpu.roll(low.astype(bf16), HALO, 1))
-
-            def tile(parts, t):
-                value = 0
-                if t > 0:
-                    value = parts[t - 1] * within(0, HALO)
-                if t < BLOCKS:
-                    value = value + parts[t] * within(HALO, LANES)
-                return value
-
-            highs = [tile(highs, t) for t in range(BLOCKS + 1)]
-            lows = [tile(lows, t) for t in range(BLOCKS + 1)]
-            for t in range(BLOCKS):
-                ext_high[n, f, t] = highs[t]
-                ext_low[n, f, t] = lows[t]
-                ext_tail[n, f, t] = (
-                    highs[t + 1] * within(0, 16)
-                    + pltpu.roll(lows[t + 1], 16, 1) * within(16, 32)
-                    + pltpu.roll(highs[t + 1], 32, 1) * within(32, 48)
-                )
-
-    def spread(half, parity, n, target):
-        spread_high, spread_low, spread_tail, _, ext_high, ext_low, ext_tail = pairs[parity]
-        e = 2 * n + parity
+    def filters(which, b, e):
+        taps = jnp.broadcast_to(base[which, pl.ds(b * EPOCHS + e, 1), :], (16, LANES))
+        return pltpu.roll(taps, 0, 1, stride=1, stride_axis=0).astype(bf16)
+
+    near_row = []
+    for g in range(2):
+        apart = lane16 % ROWS - lax.broadcasted_iota(jnp.int32, (16, LANES), 0) - 16 * g
+        near_row.append(jnp.where((apart <= 8) & (apart >= -8), 1.0, 0.0).astype(bf16))
+
+    def band_of(b, e):
+        taps = filters(0, b, e)
+        groups = [
+            pltpu.roll(taps, 8 - dith[0, e] + (16 * g - HALF - 8) % LANES, 1) * near_row[g]
+            for g in range(2)
+        ]
+        return jnp.concatenate(groups, axis=0)[:, 0 : 3 * ROWS]
+
+    def toeplitz_of(b, e):
+        taps = filters(1, b, e)
+        turned = [
+            pltpu.roll(taps, dith[1, e] + (16 * g - HALO - HALF) % LANES, 1) for g in range(8)
+        ]
+        windows = [within(max(0, 16 * g - 16), 16 * g + 16, lane16) for g in range(8)]
+        high = [turned[g] * windows[g] for g in range(8)]
+        low = [turned[(g + 4) % 8] * windows[g] for g in range(8)]
+        tail_high, tail_low = (turned[g] * within(112, LANES, lane16) for g in (0, 4))
+        return jnp.concatenate(high + high + low + [tail_high, tail_high, tail_low], axis=0)
+
+    def spread(half, e, target):
         highs, lows, tails = [], [], []
         for f in range(2):
+            cache = {}
+
+            def turned(t):
+                if t < 0:
+                    return pltpu.roll(edge[0, f], (LANES - HALO * e) % LANES, 1)
+                if t == BLOCKS:
+                    return pltpu.roll(edge[1, f], (LANES + HALO - HALO * e) % LANES, 1)
+                if t not in cache:
+                    cache[t] = pltpu.roll(fields[f][e, :, t * LANES : (t + 1) * LANES], HALO, 1)
+                return cache[t]
+
+            def tile(t):
+                if (t, 0) not in cache:
+                    high, low = split(jnp.where(lane < HALO, turned(t - 1), turned(t)))
+                    cache[t, 0] = high, low.astype(bf16)
+                return cache[t, 0]
+
             for k in HALVES[half]:
-                high, low, tail = ext_high[n, f, k], ext_low[n, f, k], ext_tail[n, f, k]
-                if k == 0:
-                    turn = (LANES - HALO * e) % LANES
-                    high = high + pltpu.roll(edge[0, 0, f], turn, 1) * within(0, HALO)
-                    low = low + pltpu.roll(edge[0, 1, f], turn, 1) * within(0, HALO)
-                if k == BLOCKS - 1:
-                    for part, to in ((0, 8), (1, 24), (0, 40)):
-                        turn = (LANES + to - HALO * e) % LANES
-                        tail = tail + pltpu.roll(edge[1, part, f], turn, 1) * within(to, to + HALO)
+                high, low = tile(k)
                 highs.append(high)
                 lows.append(low)
-                tails.append(tail)
+                high, low = tile(k + 1)
+                tails.append(
+                    high * within(0, 16)
+                    + pltpu.roll(low, 16, 1) * within(16, 32)
+                    + pltpu.roll(high, 32, 1) * within(32, 48)
+                )
         highs, lows, tails = (jnp.concatenate(parts, axis=0) for parts in (highs, lows, tails))
         data = jnp.concatenate([highs, lows, highs, tails], axis=1)
-        cols = []
-        for b in range(BASES):
-            high = spread_high[n, b]
-            cols.append(jnp.concatenate([high, high, spread_low[n, b], spread_tail[n, b]], axis=0))
-        taps = jnp.concatenate(cols, axis=1)
+        taps = jnp.concatenate([toeplitz_of(b, e) for b in range(BASES)], axis=1)
         result = jnp.dot(data[:, 0 : taps.shape[0]], taps, preferred_element_type=f32)
         high, low = split(result)
         low = low.astype(bf16)
@@ -272,15 +233,13 @@
                 target[0, b, i] = high[rows, lanes]
                 target[1, b, i] = low[rows, lanes]
 
-    def finish(half, parity, n, source):
-        band = pairs[parity][3]
-        e = 2 * n + parity
+    def finish(half, e, source):
         total = [None] * 4
         for b in range(BASES):
             high = jnp.concatenate([source[0, b, i] for i in range(4)], axis=1)
             low = jnp.concatenate([source[1, b, i] for i in range(4)], axis=1)
             smeared = jnp.dot(
-                band[n, b][:, 0 : 3 * ROWS],
+                band_of(b, e),
                 jnp.concatenate([high, low, high], axis=0),
                 preferred_element_type=f32,
             )
@@ -294,26 +253,34 @@
             val[half, e, 0, i] = weight * total[i]
             val[half, e, 1, i] = weight
 
-    def smear(half):
-        def prepare(parity, n):
-            if half == 0:
-                build(parity, n)
-                extend(parity, n)
-
+    def send_halos():
+        pl.semaphore_wait(barrier, 2 + len(offsets))
+        halo_copies = []
+        for side, target in ((0, left), (1, right)):
+            copy = pltpu.make_async_remote_copy(
+                src_ref=pack.at[side],
+                dst_ref=halo.at[side],
+                send_sem=halo_send.at[side],
+                recv_sem=halo_recv.at[side],
+                device_id=(me, target),
+                device_id_type=MESH,
+            )
+            copy.start()
+            halo_copies.append(copy)
+        return halo_copies
+
+    def smear(half, start, stop):
         def step(n, _):
-            later = (n + 1) % (EPOCHS // 2)
-            spread(half, 1, n, col1)
-            prepare(0, later)
-            finish(half, 0, n, col0)
-            spread(half, 0, later, col0)
-            prepare(1, later)
-            finish(half, 1, n, col1)
+            e = 2 * n
+            spread(half, e + 1, col1)
+            finish(half, e, col0)
+            spread(half, (e + 2) % EPOCHS, col0)
+            finish(half, e + 1, col1)
             return 0
 
-        prepare(0, 0)
-        prepare(1, 0)
-        spread(half, 0, 0, col0)
-        lax.fori_loop(0, EPOCHS // 2, step, 0)
+        if start == 0:
+            spread(half, 0, col0)
+        lax.fori_loop(start, stop, step, 0)
 
     def select(half, index, _):
         f, i = index // (2 * SIDE), index // SIDE % 2
@@ -406,18 +373,17 @@
         final[me, half] = total - sum_tree(low) - sum_tree(high)
 
     loads[5].wait()
-    smear(0)
+    smear(0, 0, 2)
+    halo_copies = send_halos()
+    smear(0, 2, EPOCHS // 2)
     lax.fori_loop(0, PEERS, lambda index, _: select(0, index, _), 0, unroll=2)
     near0 = send_near(0)
     for copy in halo_copies:
         copy.wait_recv()
     for side, at_end in ((0, 0), (1, strips - 1)):
         for f in range(2):
-            value = halo[1 - side, f] * jnp.where(sky == at_end, 0.0, 1.0)
-            high, low = split(value)
-            edge[side, 0, f] = high
-            edge[side, 1, f] = low.astype(bf16)
-    smear(1)
+            edge[side, f] = halo[1 - side, f] * jnp.where(sky == at_end, 0.0, 1.0)
+    smear(1, 0, EPOCHS // 2)
     lax.fori_loop(0, PEERS, lambda index, _: select(1, index, _), 0, unroll=2)
     near1 = send_near(1)
     far0 = send_far(0, near0)
@@ -458,7 +424,7 @@
     trimmed = pl.pallas_call(
         kernel,
         out_shape=jax.ShapeDtypeStruct((2, ROWS, BLOCKS * LANES), f32),
-        in_specs=[pl.BlockSpec(memory_space=pl.ANY)] * 6,
+        in_specs=[pl.BlockSpec(memory_space=pltpu.HBM)] * 6,
         out_specs=pl.BlockSpec(memory_space=pltpu.VMEM),
         scratch_shapes=[
             vmem((EPOCHS, ROWS, BLOCKS * LANES), f32),
@@ -468,22 +434,10 @@
             vmem((TAPS, BASES, EPOCHS), f32),
             pltpu.SMEM((2, EPOCHS), jnp.int32),
             vmem((LANES, LANES), f32),
-            vmem((4, EPOCHS * BASES * 8, LANES), f32),
-            *(
-                2
-                * [
-                vmem((EPOCHS // 2, BASES, LANES, LANES), bf16),
-                vmem((EPOCHS // 2, BASES, LANES, LANES), bf16),
-                vmem((EPOCHS // 2, BASES, 48, LANES), bf16),
-                vmem((EPOCHS // 2, BASES, ROWS, LANES), bf16),
-                vmem((EPOCHS // 2, 2, BLOCKS, ROWS, LANES), bf16),
-                vmem((EPOCHS // 2, 2, BLOCKS, ROWS, LANES), bf16),
-                vmem((EPOCHS // 2, 2, BLOCKS, ROWS, LANES), bf16),
-                ]
-            ),
+            vmem((2, EPOCHS * BASES, LANES), f32),
             vmem((2, 2, ROWS, LANES), f32),
             vmem((2, 2, ROWS, LANES), f32),
-            vmem((2, 2, 2, ROWS, LANES), bf16),
+            vmem((2, 2, ROWS, LANES), f32),
             vmem((2, BASES, 4, ROWS, LANES), bf16),
             vmem((2, BASES, 4, ROWS, LANES), bf16),
             vmem((2, EPOCHS, 2, 2, ROWS, LANES), f32),

time: 39.9 us -> 37.8 us (0.947)
  Pallas kernels: 37.6 us -> 35.3 us
    pallas_call x1, Pallas kernels: 37.6 us -> 35.3 us  [per_device(): pl.pallas_call(kernel, out_shape=jax.ShapeDtypeStruct((2, ROWS, BLOCKS *...]
where the time goes in v3:
time: 37.8 us; the launch traced here: 37.4 us
  Pallas kernels  35.3 us (93%)
  other arithmetic  1.53 us (4%)
  between operations  0.64 us (2%)
    pallas_call x1, Pallas kernels, per_device(): pl.pallas_call(kernel, out_shape=jax.ShapeDtypeStruct((2, ROWS, BLOCKS *...  35.3 us
    div x1, other arithmetic, per_device(): return (trimmed[0] / trimmed[1], trimmed[1] / kept_count)  1.53 us

profile of v3, /device:TPU:2, one launch (start us, length us, event | category | flops | bytes accessed | tf_op | source)
XLA Modules:
  0.0 37.4 jit_solution(14022782420254091033)
XLA Ops:
  0.6 35.3 %coadd.1 = f32[2,32,512]{2,1,0:T(8,128)} custom-call(f32[16,32,512]{2,1,0:T(8,128)} %img_hbm.1, f32[16,32,512]{2,1,0:T(8,128)} %var_hbm.1, bf16[16,4,32,512]{3,2,1,0:T(8,128)(2,1)} %coef_hbm.1, f32[11,4,16]{2,1,0:T(4,128)} %bitcast.7, f32[11,4,16]{2,1,0:T(4,128)} %bitcast.8, s32[2,16]{1,0:T(2,128)} %bitcast.9), custom_call_target="tpu_custom_call" | custom-call | tf_op jit(solution)/shard_map/coadd/pallas_call | solution.py:424
  35.9 1.5 %multiply_bitcast_fusion = (f32[32,512]{1,0:T(8,128)}, f32[32,512]{1,0:T(8,128)}) fusion(f32[2,32,512]{2,1,0:T(8,128)} %coadd.1), kind=kLoop, calls=%fused_computation | loop fusion | flops 32768 | bytes 262144 | tf_op jit(solution)/shard_map/div | solution.py:475

commit v4 on v3

--- a/solution.py
+++ b/solution.py
@@ -14,6 +14,7 @@
 
 LANES = 128
 EPOCHS = 16
+FIRST = 6
 ROWS = 32
 BLOCKS = 4
 SIDE = 4
@@ -79,7 +80,7 @@
 
 def kernel(
     img_hbm, var_hbm, coef_hbm, rowf_hbm, colf_hbm, dith_hbm, out_ref,
-    img, var, coef, rowf, colf, dith, filt, base, pack, halo, edge, col0, col1, val, lists,
+    img, var, coef, rowf, colf, dith, filt, base, pack, halo, edge, col0, col1, col2, col3, val, lists,
     near_low, near_high, mid_low, mid_high, far_low, far_high, final,
     in_sem, halo_send, halo_recv, near_send, near_recv, far_send, far_recv, fin_send, fin_recv,
 ):
@@ -98,18 +99,16 @@
 
     loads = [
         pltpu.make_async_copy(source, target, in_sem.at[i])
-        for i, (source, target) in enumerate(
-            (
-                (rowf_hbm, rowf),
-                (colf_hbm, colf),
-                (dith_hbm, dith),
-                (img_hbm, img),
-                (var_hbm, var),
-                (coef_hbm, coef),
-            )
-        )
+        for i, (source, target) in enumerate(((rowf_hbm, rowf), (colf_hbm, colf), (dith_hbm, dith)))
     ]
-    for load in loads:
+    portions = []
+    for start, count in ((0, FIRST), (FIRST, EPOCHS - FIRST)):
+        rows, part = pl.ds(start, count), []
+        for source, target in ((img_hbm, img), (var_hbm, var), (coef_hbm, coef)):
+            sem = in_sem.at[3 + 3 * len(portions) + len(part)]
+            part.append(pltpu.make_async_copy(source.at[rows], target.at[rows], sem))
+        portions.append(part)
+    for load in loads + portions[0] + portions[1]:
         load.start()
 
     barrier = pltpu.get_barrier_semaphore()
@@ -145,8 +144,6 @@
                 parts = high + pltpu.roll(low, 64, 1)
             base[kind, b * EPOCHS : (b + 1) * EPOCHS, :] = parts
 
-    loads[3].wait()
-    loads[4].wait()
     fields = (img, var)
     last_cols = slice((BLOCKS - 1) * LANES, BLOCKS * LANES)
 
@@ -159,8 +156,6 @@
             pack[1, f] = jnp.where(mine, last, pack[1, f])
         return 0
 
-    lax.fori_loop(0, EPOCHS, gather_edges, 0, unroll=4)
-
     loads[2].wait()
 
     def filters(which, b, e):
@@ -180,46 +175,41 @@
         ]
         return jnp.concatenate(groups, axis=0)[:, 0 : 3 * ROWS]
 
+    row16 = lax.broadcasted_iota(jnp.int32, (16, LANES), 0)
+    before = jnp.where((row16 >= 8) & (lane16 < 8), 1.0, 0.0).astype(bf16)
+    after = jnp.where((row16 < 8) & (lane16 >= LANES - 8), 1.0, 0.0).astype(bf16)
+
     def toeplitz_of(b, e):
         taps = filters(1, b, e)
-        turned = [
-            pltpu.roll(taps, dith[1, e] + (16 * g - HALO - HALF) % LANES, 1) for g in range(8)
-        ]
-        windows = [within(max(0, 16 * g - 16), 16 * g + 16, lane16) for g in range(8)]
+        turned = [pltpu.roll(taps, dith[1, e] + (16 * g - HALF) % LANES, 1) for g in range(8)]
+        windows = [within(max(0, 16 * g - 8), 16 * g + 24, lane16) for g in range(8)]
         high = [turned[g] * windows[g] for g in range(8)]
         low = [turned[(g + 4) % 8] * windows[g] for g in range(8)]
-        tail_high, tail_low = (turned[g] * within(112, LANES, lane16) for g in (0, 4))
-        return jnp.concatenate(high + high + low + [tail_high, tail_high, tail_low], axis=0)
+        before_high, before_low = turned[7] * before, turned[3] * before
+        after_high, after_low = turned[0] * after, turned[4] * after
+        sides = [before_high, after_high + before_high, after_high + before_low, after_low]
+        return jnp.concatenate(high + high + low + sides, axis=0)
 
     def spread(half, e, target):
         highs, lows, tails = [], [], []
         for f in range(2):
-            cache = {}
-
-            def turned(t):
+
+            def tile(t):
                 if t < 0:
-                    return pltpu.roll(edge[0, f], (LANES - HALO * e) % LANES, 1)
+                    return pltpu.roll(edge[0, f], (2 * LANES - HALO - HALO * e) % LANES, 1)
                 if t == BLOCKS:
-                    return pltpu.roll(edge[1, f], (LANES + HALO - HALO * e) % LANES, 1)
-                if t not in cache:
-                    cache[t] = pltpu.roll(fields[f][e, :, t * LANES : (t + 1) * LANES], HALO, 1)
-                return cache[t]
-
-            def tile(t):
-                if (t, 0) not in cache:
-                    high, low = split(jnp.where(lane < HALO, turned(t - 1), turned(t)))
-                    cache[t, 0] = high, low.astype(bf16)
-                return cache[t, 0]
+                    return pltpu.roll(edge[1, f], (LANES - HALO * e) % LANES, 1)
+                return fields[f][e, :, t * LANES : (t + 1) * LANES]
 
             for k in HALVES[half]:
-                high, low = tile(k)
+                high, low = split(tile(k))
                 highs.append(high)
-                lows.append(low)
-                high, low = tile(k + 1)
+                lows.append(low.astype(bf16))
+                high, low = split(jnp.where(lane < HALO, tile(k + 1), tile(k - 1)))
                 tails.append(
-                    high * within(0, 16)
-                    + pltpu.roll(low, 16, 1) * within(16, 32)
-                    + pltpu.roll(high, 32, 1) * within(32, 48)
+                    pltpu.roll(high, 16, 1) * within(8, 24)
+                    + pltpu.roll(low.astype(bf16), 32, 1) * within(24, 40)
+                    + pltpu.roll(high, 48, 1) * within(40, 56)
                 )
         highs, lows, tails = (jnp.concatenate(parts, axis=0) for parts in (highs, lows, tails))
         data = jnp.concatenate([highs, lows, highs, tails], axis=1)
@@ -254,6 +244,7 @@
             val[half, e, 1, i] = weight
 
     def send_halos():
+        lax.fori_loop(0, EPOCHS, gather_edges, 0, unroll=4)
         pl.semaphore_wait(barrier, 2 + len(offsets))
         halo_copies = []
         for side, target in ((0, left), (1, right)):
@@ -271,15 +262,20 @@
 
     def smear(half, start, stop):
         def step(n, _):
-            e = 2 * n
-            spread(half, e + 1, col1)
+            e = 4 * n
+            spread(half, e + 2, col2)
             finish(half, e, col0)
-            spread(half, (e + 2) % EPOCHS, col0)
+            spread(half, e + 3, col3)
             finish(half, e + 1, col1)
+            spread(half, (e + 4) % EPOCHS, col0)
+            finish(half, e + 2, col2)
+            spread(half, (e + 5) % EPOCHS, col1)
+            finish(half, e + 3, col3)
             return 0
 
         if start == 0:
             spread(half, 0, col0)
+            spread(half, 1, col1)
         lax.fori_loop(start, stop, step, 0)
 
     def select(half, index, _):
@@ -372,10 +368,13 @@
         total = sum_tree([part[REJECT] for part in highs])
         final[me, half] = total - sum_tree(low) - sum_tree(high)
 
-    loads[5].wait()
-    smear(0, 0, 2)
+    for load in portions[0]:
+        load.wait()
+    smear(0, 0, 1)
+    for load in portions[1]:
+        load.wait()
     halo_copies = send_halos()
-    smear(0, 2, EPOCHS // 2)
+    smear(0, 1, EPOCHS // 4)
     lax.fori_loop(0, PEERS, lambda index, _: select(0, index, _), 0, unroll=2)
     near0 = send_near(0)
     for copy in halo_copies:
@@ -383,7 +382,7 @@
     for side, at_end in ((0, 0), (1, strips - 1)):
         for f in range(2):
             edge[side, f] = halo[1 - side, f] * jnp.where(sky == at_end, 0.0, 1.0)
-    smear(1, 0, EPOCHS // 2)
+    smear(1, 0, EPOCHS // 4)
     lax.fori_loop(0, PEERS, lambda index, _: select(1, index, _), 0, unroll=2)
     near1 = send_near(1)
     far0 = send_far(0, near0)
@@ -440,6 +439,8 @@
             vmem((2, 2, ROWS, LANES), f32),
             vmem((2, BASES, 4, ROWS, LANES), bf16),
             vmem((2, BASES, 4, ROWS, LANES), bf16),
+            vmem((2, BASES, 4, ROWS, LANES), bf16),
+            vmem((2, BASES, 4, ROWS, LANES), bf16),
             vmem((2, EPOCHS, 2, 2, ROWS, LANES), f32),
             vmem((2, LISTS, SIDE, SIDE) + tile, f32),
             vmem((2, SIDE - 1, REJECT, SIDE) + tile, f32),
@@ -449,7 +450,7 @@
             vmem((2, SIDE - 1, REJECT) + tile, f32),
             vmem((2, SIDE - 1, REJECT + 1) + tile, f32),
             vmem((PEERS, 2) + tile, f32),
-            dma((6,)),
+            dma((9,)),
             dma((2,)),
             dma((2,)),
             dma((2, 2, SIDE - 1)),

time: 37.8 us -> 35.6 us (0.942)
  Pallas kernels: 35.3 us -> 33.3 us
    pallas_call x1, Pallas kernels: 35.3 us -> 33.3 us  [per_device(): pl.pallas_call(kernel, out_shape=jax.ShapeDtypeStruct((2, ROWS, BLOCKS *...]
where the time goes in v4:
time: 35.6 us; the launch traced here: 35.5 us
  Pallas kernels  33.3 us (94%)
  other arithmetic  1.53 us (4%)
  between operations  0.64 us (2%)
    pallas_call x1, Pallas kernels, per_device(): pl.pallas_call(kernel, out_shape=jax.ShapeDtypeStruct((2, ROWS, BLOCKS *...  33.3 us
    div x1, other arithmetic, per_device(): return (trimmed[0] / trimmed[1], trimmed[1] / kept_count)  1.53 us

profile of v4, /device:TPU:2, one launch (start us, length us, event | category | flops | bytes accessed | tf_op | source)
XLA Modules:
  0.0 35.5 jit_solution(819176948550945513)
XLA Ops:
  0.6 33.3 %coadd.1 = f32[2,32,512]{2,1,0:T(8,128)} custom-call(f32[16,32,512]{2,1,0:T(8,128)} %img_hbm.1, f32[16,32,512]{2,1,0:T(8,128)} %var_hbm.1, bf16[16,4,32,512]{3,2,1,0:T(8,128)(2,1)} %coef_hbm.1, f32[11,4,16]{2,1,0:T(4,128)} %bitcast.7, f32[11,4,16]{2,1,0:T(4,128)} %bitcast.8, s32[2,16]{1,0:T(2,128)} %bitcast.9), custom_call_target="tpu_custom_call" | custom-call | tf_op jit(solution)/shard_map/coadd/pallas_call | solution.py:423
  33.9 1.5 %multiply_bitcast_fusion = (f32[32,512]{1,0:T(8,128)}, f32[32,512]{1,0:T(8,128)}) fusion(f32[2,32,512]{2,1,0:T(8,128)} %coadd.1), kind=kLoop, calls=%fused_computation | loop fusion | flops 32768 | bytes 262144 | tf_op jit(solution)/shard_map/div | solution.py:476

commit v5 on v4

--- a/solution.py
+++ b/solution.py
@@ -15,6 +15,7 @@
 LANES = 128
 EPOCHS = 16
 FIRST = 6
+STEPS = EPOCHS // 4
 ROWS = 32
 BLOCKS = 4
 SIDE = 4
@@ -81,8 +82,8 @@
 def kernel(
     img_hbm, var_hbm, coef_hbm, rowf_hbm, colf_hbm, dith_hbm, out_ref,
     img, var, coef, rowf, colf, dith, filt, base, pack, halo, edge, col0, col1, col2, col3, val, lists,
-    near_low, near_high, mid_low, mid_high, far_low, far_high, final,
-    in_sem, halo_send, halo_recv, near_send, near_recv, far_send, far_recv, fin_send, fin_recv,
+    near_low, near_high, mid_low, mid_high, far_low, far_high, direct, final,
+    in_sem, halo_send, halo_recv, near_send, near_recv, far_send, far_recv, dir_send, dir_recv, fin_send, fin_recv,
 ):
     f32, bf16 = jnp.float32, jnp.bfloat16
     me = lax.axis_index("epoch")
@@ -260,23 +261,20 @@
             halo_copies.append(copy)
         return halo_copies
 
+    buffers = (col0, col1, col2, col3)
+
+    def step(half, n, ahead=None):
+        e = 4 * n
+        ahead = [(half, e + 4), (half, e + 5)] if ahead is None else ahead
+        columns = [(half, e + 2), (half, e + 3), *ahead]
+        for i in range(4):
+            finish(half, e + i, buffers[i])
+            if i < len(columns):
+                spread(*columns[i], buffers[(i + 2) % 4])
+        return 0
+
     def smear(half, start, stop):
-        def step(n, _):
-            e = 4 * n
-            spread(half, e + 2, col2)
-            finish(half, e, col0)
-            spread(half, e + 3, col3)
-            finish(half, e + 1, col1)
-            spread(half, (e + 4) % EPOCHS, col0)
-            finish(half, e + 2, col2)
-            spread(half, (e + 5) % EPOCHS, col1)
-            finish(half, e + 3, col3)
-            return 0
-
-        if start == 0:
-            spread(half, 0, col0)
-            spread(half, 1, col1)
-        lax.fori_loop(start, stop, step, 0)
+        lax.fori_loop(start, stop, lambda n, _: step(half, n), 0)
 
     def select(half, index, _):
         f, i = index // (2 * SIDE), index // SIDE % 2
@@ -355,6 +353,34 @@
             result += [low, high]
         return result
 
+    def send_direct(half):
+        copies = []
+        for i, (dy, dx) in enumerate(offsets):
+            x, y = (my_x + dx) % SIDE, (my_y + dy) % SIDE
+            copies.append(
+                copy_to(
+                    lists.at[half, :, x, y], direct.at[i], dir_send.at[i], dir_recv.at[i], dy, dx
+                )
+            )
+        return copies
+
+    def close_direct(half, copies):
+        ends = []
+        for f, pick in ((0, lower_four), (1, upper_four)):
+            rows = range(f * REJECT, (f + 1) * REJECT)
+            parts = [[lists[half, i, my_x, my_y] for i in rows]]
+            for n, copy in enumerate(copies):
+                if f == 0:
+                    copy.wait_recv()
+                parts.append([direct[n, i] for i in rows])
+            while len(parts) > 2:
+                parts = [sort_bitonic(pick(parts[i], parts[i + 1])) for i in range(0, len(parts), 2)]
+            ends += pick(*parts)
+        total = sum_tree(
+            [lists[half, 2 * REJECT, my_x, my_y]] + [direct[n, 2 * REJECT] for n in range(len(copies))]
+        )
+        final[me, half] = total - sum_tree(ends)
+
     def close(half, copies):
         for copy in copies:
             copy.wait_recv()
@@ -370,11 +396,14 @@
 
     for load in portions[0]:
         load.wait()
-    smear(0, 0, 1)
+    spread(0, 0, col0)
+    spread(0, 1, col1)
+    step(0, 0)
     for load in portions[1]:
         load.wait()
     halo_copies = send_halos()
-    smear(0, 1, EPOCHS // 4)
+    smear(0, 1, STEPS - 1)
+    step(0, STEPS - 1, [])
     lax.fori_loop(0, PEERS, lambda index, _: select(0, index, _), 0, unroll=2)
     near0 = send_near(0)
     for copy in halo_copies:
@@ -382,13 +411,15 @@
     for side, at_end in ((0, 0), (1, strips - 1)):
         for f in range(2):
             edge[side, f] = halo[1 - side, f] * jnp.where(sky == at_end, 0.0, 1.0)
-    smear(1, 0, EPOCHS // 4)
+    spread(1, 0, col0)
+    spread(1, 1, col1)
+    smear(1, 0, STEPS - 1)
+    step(1, STEPS - 1, [])
     lax.fori_loop(0, PEERS, lambda index, _: select(1, index, _), 0, unroll=2)
-    near1 = send_near(1)
+    direct1 = send_direct(1)
     far0 = send_far(0, near0)
-    far1 = send_far(1, near1)
     close(0, far0)
-    close(1, far1)
+    close_direct(1, direct1)
 
     copies = [
         copy_to(final.at[me], final.at[me], fin_send.at[i], fin_recv.at[i], dy, dx)
@@ -412,7 +443,7 @@
                 (unit % SIDE) * SIDE + unit // SIDE, half
             ]
 
-    for copy in halo_copies + near0 + near1 + far0 + far1 + copies:
+    for copy in halo_copies + near0 + far0 + direct1 + copies:
         copy.wait_send()
 
 
@@ -449,6 +480,7 @@
             vmem((2, REJECT + 1, SIDE) + tile, f32),
             vmem((2, SIDE - 1, REJECT) + tile, f32),
             vmem((2, SIDE - 1, REJECT + 1) + tile, f32),
+            vmem((PEERS - 1, LISTS) + tile, f32),
             vmem((PEERS, 2) + tile, f32),
             dma((9,)),
             dma((2,)),
@@ -457,6 +489,8 @@
             dma((2, 2, SIDE - 1)),
             dma((2, 2, SIDE - 1)),
             dma((2, 2, SIDE - 1)),
+            dma((PEERS - 1,)),
+            dma((PEERS - 1,)),
             dma((PEERS - 1,)),
             dma((PEERS - 1,)),
         ],

time: 35.6 us -> 34.3 us (0.963)
  Pallas kernels: 33.3 us -> 31.9 us
    pallas_call x1, Pallas kernels: 33.3 us -> 31.9 us  [per_device(): pl.pallas_call(kernel, out_shape=jax.ShapeDtypeStruct((2, ROWS, BLOCKS *...]
where the time goes in v5:
time: 34.3 us; the launch traced here: 34.1 us
  Pallas kernels  31.9 us (93%)
  other arithmetic  1.53 us (4%)
  between operations  0.64 us (2%)
    pallas_call x1, Pallas kernels, per_device(): pl.pallas_call(kernel, out_shape=jax.ShapeDtypeStruct((2, ROWS, BLOCKS *...  31.9 us
    div x1, other arithmetic, per_device(): return (trimmed[0] / trimmed[1], trimmed[1] / kept_count)  1.53 us

profile of v5, /device:TPU:2, one launch (start us, length us, event | category | flops | bytes accessed | tf_op | source)
XLA Modules:
  0.0 34.1 jit_solution(3125586042959512884)
XLA Ops:
  0.6 31.9 %coadd.1 = f32[2,32,512]{2,1,0:T(8,128)} custom-call(f32[16,32,512]{2,1,0:T(8,128)} %img_hbm.1, f32[16,32,512]{2,1,0:T(8,128)} %var_hbm.1, bf16[16,4,32,512]{3,2,1,0:T(8,128)(2,1)} %coef_hbm.1, f32[11,4,16]{2,1,0:T(4,128)} %bitcast.7, f32[11,4,16]{2,1,0:T(4,128)} %bitcast.8, s32[2,16]{1,0:T(2,128)} %bitcast.9), custom_call_target="tpu_custom_call" | custom-call | tf_op jit(solution)/shard_map/coadd/pallas_call | solution.py:454
  32.6 1.5 %multiply_bitcast_fusion = (f32[32,512]{1,0:T(8,128)}, f32[32,512]{1,0:T(8,128)}) fusion(f32[2,32,512]{2,1,0:T(8,128)} %coadd.1), kind=kLoop, calls=%fused_computation | loop fusion | flops 32768 | bytes 262144 | tf_op jit(solution)/shard_map/div | solution.py:510

commit v6 on v5

--- a/solution.py
+++ b/solution.py
@@ -245,7 +245,7 @@
             val[half, e, 1, i] = weight
 
     def send_halos():
-        lax.fori_loop(0, EPOCHS, gather_edges, 0, unroll=4)
+        lax.fori_loop(0, EPOCHS, gather_edges, 0, unroll=16)
         pl.semaphore_wait(barrier, 2 + len(offsets))
         halo_copies = []
         for side, target in ((0, left), (1, right)):
@@ -404,7 +404,7 @@
     halo_copies = send_halos()
     smear(0, 1, STEPS - 1)
     step(0, STEPS - 1, [])
-    lax.fori_loop(0, PEERS, lambda index, _: select(0, index, _), 0, unroll=2)
+    lax.fori_loop(0, PEERS, lambda index, _: select(0, index, _), 0, unroll=4)
     near0 = send_near(0)
     for copy in halo_copies:
         copy.wait_recv()
@@ -415,7 +415,7 @@
     spread(1, 1, col1)
     smear(1, 0, STEPS - 1)
     step(1, STEPS - 1, [])
-    lax.fori_loop(0, PEERS, lambda index, _: select(1, index, _), 0, unroll=2)
+    lax.fori_loop(0, PEERS, lambda index, _: select(1, index, _), 0, unroll=4)
     direct1 = send_direct(1)
     far0 = send_far(0, near0)
     close(0, far0)

time: 34.3 us -> 34 us (level)
  no operation moved by 1% of the time
where the time goes in v6:
time: 34 us; the launch traced here: 33.8 us
  Pallas kernels  31.7 us (93%)
  other arithmetic  1.53 us (4%)
  between operations  0.64 us (2%)
    pallas_call x1, Pallas kernels, per_device(): pl.pallas_call(kernel, out_shape=jax.ShapeDtypeStruct((2, ROWS, BLOCKS *...  31.7 us
    div x1, other arithmetic, per_device(): return (trimmed[0] / trimmed[1], trimmed[1] / kept_count)  1.53 us

profile of v6, /device:TPU:2, one launch (start us, length us, event | category | flops | bytes accessed | tf_op | source)
XLA Modules:
  0.0 33.8 jit_solution(12356900368571001853)
XLA Ops:
  0.6 31.7 %coadd.1 = f32[2,32,512]{2,1,0:T(8,128)} custom-call(f32[16,32,512]{2,1,0:T(8,128)} %img_hbm.1, f32[16,32,512]{2,1,0:T(8,128)} %var_hbm.1, bf16[16,4,32,512]{3,2,1,0:T(8,128)(2,1)} %coef_hbm.1, f32[11,4,16]{2,1,0:T(4,128)} %bitcast.7, f32[11,4,16]{2,1,0:T(4,128)} %bitcast.8, s32[2,16]{1,0:T(2,128)} %bitcast.9), custom_call_target="tpu_custom_call" | custom-call | tf_op jit(solution)/shard_map/coadd/pallas_call | solution.py:454
  32.3 1.5 %multiply_bitcast_fusion = (f32[32,512]{1,0:T(8,128)}, f32[32,512]{1,0:T(8,128)}) fusion(f32[2,32,512]{2,1,0:T(8,128)} %coadd.1), kind=kLoop, calls=%fused_computation | loop fusion | flops 32768 | bytes 262144 | tf_op jit(solution)/shard_map/div | solution.py:510

commit v7 on v6

--- a/solution.py
+++ b/solution.py
@@ -365,20 +365,23 @@
         return copies
 
     def close_direct(half, copies):
-        ends = []
-        for f, pick in ((0, lower_four), (1, upper_four)):
-            rows = range(f * REJECT, (f + 1) * REJECT)
-            parts = [[lists[half, i, my_x, my_y] for i in rows]]
-            for n, copy in enumerate(copies):
-                if f == 0:
-                    copy.wait_recv()
-                parts.append([direct[n, i] for i in rows])
-            while len(parts) > 2:
-                parts = [sort_bitonic(pick(parts[i], parts[i + 1])) for i in range(0, len(parts), 2)]
-            ends += pick(*parts)
-        total = sum_tree(
-            [lists[half, 2 * REJECT, my_x, my_y]] + [direct[n, 2 * REJECT] for n in range(len(copies))]
-        )
+        def listed(n, start, count):
+            if n < 0:
+                return [lists[half, i, my_x, my_y] for i in range(start, start + count)]
+            return [direct[n, i] for i in range(start, start + count)]
+
+        lows, highs, sums = [], [], []
+        for start in range(0, PEERS, SIDE):
+            group = [n if n < len(copies) else -1 for n in range(start, start + SIDE)]
+            for n in group:
+                if n >= 0:
+                    copies[n].wait_recv()
+            lows.append(tree([listed(n, 0, REJECT) for n in group], lower_four))
+            highs.append(tree([listed(n, REJECT, REJECT) for n in group], upper_four))
+            sums.append(sum_tree([listed(n, 2 * REJECT, 1)[0] for n in group]))
+        low = lower_four(*(sort_bitonic(lower_four(lows[i], lows[i + 1])) for i in (0, 2)))
+        high = upper_four(*(sort_bitonic(upper_four(highs[i], highs[i + 1])) for i in (0, 2)))
+        total, ends = sum_tree(sums), low + high
         final[me, half] = total - sum_tree(ends)
 
     def close(half, copies):

time: 34 us -> 34 us (level)
  no operation moved by 1% of the time
where the time goes in v7:
time: 34 us; the launch traced here: 33.8 us
  Pallas kernels  31.7 us (93%)
  other arithmetic  1.53 us (4%)
  between operations  0.64 us (2%)
    pallas_call x1, Pallas kernels, per_device(): pl.pallas_call(kernel, out_shape=jax.ShapeDtypeStruct((2, ROWS, BLOCKS *...  31.7 us
    div x1, other arithmetic, per_device(): return (trimmed[0] / trimmed[1], trimmed[1] / kept_count)  1.53 us

profile of v7, /device:TPU:2, one launch (start us, length us, event | category | flops | bytes accessed | tf_op | source)
XLA Modules:
  0.0 33.8 jit_solution(701474849638687595)
XLA Ops:
  0.6 31.7 %coadd.1 = f32[2,32,512]{2,1,0:T(8,128)} custom-call(f32[16,32,512]{2,1,0:T(8,128)} %img_hbm.1, f32[16,32,512]{2,1,0:T(8,128)} %var_hbm.1, bf16[16,4,32,512]{3,2,1,0:T(8,128)(2,1)} %coef_hbm.1, f32[11,4,16]{2,1,0:T(4,128)} %bitcast.7, f32[11,4,16]{2,1,0:T(4,128)} %bitcast.8, s32[2,16]{1,0:T(2,128)} %bitcast.9), custom_call_target="tpu_custom_call" | custom-call | tf_op jit(solution)/shard_map/coadd/pallas_call | solution.py:457
  32.3 1.5 %multiply_bitcast_fusion = (f32[32,512]{1,0:T(8,128)}, f32[32,512]{1,0:T(8,128)}) fusion(f32[2,32,512]{2,1,0:T(8,128)} %coadd.1), kind=kLoop, calls=%fused_computation | loop fusion | flops 32768 | bytes 262144 | tf_op jit(solution)/shard_map/div | solution.py:513
